TPU v7x, 256 devices: a whole 4x4x8 slice. The times are simulated.
256 devices in a mesh: row: 8 (over x_hi, y), col: 32 (over x_lo, z, core).
Axes of the slice: x: 4 (x_hi: 2, x_lo: 2; x = x_hi * 2 + x_lo), y: 4, z: 8, core: 2. Of those that a mesh axis runs over, the one named last changes fastest.
Arguments:
- object_slices: float32 [2, 2, 4096, 8192], P(None, None, 'row', 'col'), may hold values from -5 to 5
- probe_field: float32 [2, 256, 256], replicated, may hold values from -6 to 6
- scan_offsets: int32 [8, 32, 2, 4], P('row', 'col'), may hold values from 0 to 7936, as said below
- scan_count: int32 [8, 32], P('row', 'col'), may hold values from 2 to 4, as said below
- measured: float32 [8, 32, 4, 256, 256], P('row', 'col'), may hold values from 0.2 to 2
Outputs:
- object_grad: float32 [2, 2, 4096, 8192], P(None, None, 'row', 'col')
- probe_grad: float32 [2, 256, 256], replicated
Inputs may be any that keep to these rules, and one draw needn't show every extreme that they name: `scan_offsets`: for every tile and slot, the offsets are a window's first row and first column in global pixels; the window's centre (first row + 128, first column + 128) lies in that tile, and the whole window of 256 x 256 pixels lies inside the object. Slots at or beyond the tile's count hold offsets of the same kind and are not scanned. `scan_count`: some tile has all 4 slots scanned.
All inputs are finite; a program needn't handle non-finite values.
Results may differ from a plain program's by a relative error of at most 0.0003.
Values sent between devices are 32-bit elements; how exact they have to be, the bound alone decides.
A program may use at most 128 MiB of HBM per device.

v0:
```python
import math

import jax
import jax.numpy as jnp
from jax import lax
from jax.sharding import PartitionSpec as P

DEFOCUS = 0.3
FLOOR = 0.5


def with_halo(x, sides, width):
    for axis, dim in sides:
        size, length = (lax.axis_size(axis), x.shape[dim])
        up = [(i, (i + 1) % size) for i in range(size - 1)]
        down = [(j, i) for i, j in up]
        last = lax.slice_in_dim(x, length - width, length, axis=dim)
        leading = lax.slice_in_dim(x, 0, width, axis=dim)
        before = lax.ppermute(last, axis, up)
        after = lax.ppermute(leading, axis, down)
        x = jnp.concatenate([before, x, after], axis=dim)
    return x


def passed_along(block, axis, distance):
    devices = range(lax.axis_size(axis))
    route = [(i - distance, i) for i in devices if i - distance in devices]
    return lax.ppermute(block, axis, route)


def dft_tables(window):
    indices = jnp.arange(window, dtype=jnp.int32)
    product = indices[:, None] * indices[None, :] % window
    angles = product.astype(jnp.float32) * (-2.0 * math.pi / window)
    norm_scale = 1.0 / math.sqrt(window)
    return (jnp.cos(angles) * norm_scale, jnp.sin(angles) * norm_scale)


def transfer_tables(window):
    indices = jnp.arange(window, dtype=jnp.int32)
    frequency = (indices + window // 2) % window - window // 2
    radius = frequency[:, None] * frequency[:, None] + frequency[None, :] * frequency[None, :]
    phases = radius.astype(jnp.float32) * (-math.pi * DEFOCUS / window)
    return (jnp.cos(phases), jnp.sin(phases))


def transform(x_re, x_im, c_re, c_im):
    highest = lax.Precision.HIGHEST
    y_re = jnp.einsum("jk,skl->sjl", c_re, x_re, precision=highest) - jnp.einsum(
        "jk,skl->sjl", c_im, x_im, precision=highest
    )
    y_im = jnp.einsum("jk,skl->sjl", c_re, x_im, precision=highest) + jnp.einsum(
        "jk,skl->sjl", c_im, x_re, precision=highest
    )
    z_re = jnp.einsum("sjk,kl->sjl", y_re, c_re, precision=highest) - jnp.einsum(
        "sjk,kl->sjl", y_im, c_im, precision=highest
    )
    z_im = jnp.einsum("sjk,kl->sjl", y_re, c_im, precision=highest) + jnp.einsum(
        "sjk,kl->sjl", y_im, c_re, precision=highest
    )
    return (z_re, z_im)


def propagate(x_re, x_im, tables, conjugate):
    c_re, c_im, h_re, h_im = tables
    if conjugate:
        h_im = -h_im
    f_re, f_im = transform(x_re, x_im, c_re, c_im)
    m_re = h_re * f_re - h_im * f_im
    m_im = h_re * f_im + h_im * f_re
    return transform(m_re, m_im, c_re, -c_im)


def slot_gradients(patches, probe_field, amplitudes, live_mask):
    layers = patches.shape[1]
    window = probe_field.shape[1]
    c_re, c_im = dft_tables(window)
    h_re, h_im = transfer_tables(window)
    tables = (c_re, c_im, h_re, h_im)
    cur_re = jnp.broadcast_to(probe_field[0], patches[:, 0, 0].shape)
    cur_im = jnp.broadcast_to(probe_field[1], patches[:, 0, 0].shape)
    saved = []
    for layer in range(layers):
        t_re = patches[:, layer, 0]
        t_im = patches[:, layer, 1]
        saved.append((cur_re, cur_im))
        e_re = t_re * cur_re - t_im * cur_im
        e_im = t_re * cur_im + t_im * cur_re
        if layer < layers - 1:
            cur_re, cur_im = propagate(e_re, e_im, tables, False)
    far_re, far_im = transform(e_re, e_im, c_re, c_im)
    magnitude = jnp.sqrt(far_re * far_re + far_im * far_im)
    weight = live_mask[:, None, None] * (1.0 - amplitudes / jnp.maximum(magnitude, FLOOR))
    back_re, back_im = transform(weight * far_re, weight * far_im, c_re, -c_im)
    layer_grads = []
    for layer in range(layers - 1, -1, -1):
        psi_re, psi_im = saved[layer]
        t_re = patches[:, layer, 0]
        t_im = patches[:, layer, 1]
        grad_re = psi_re * back_re + psi_im * back_im
        grad_im = psi_re * back_im - psi_im * back_re
        layer_grads.append(jnp.stack([grad_re, grad_im], axis=1))
        q_re = t_re * back_re + t_im * back_im
        q_im = t_re * back_im - t_im * back_re
        if layer > 0:
            back_re, back_im = propagate(q_re, q_im, tables, True)
    patch_grads = jnp.stack(layer_grads[::-1], axis=1)
    probe_term = jnp.stack([jnp.sum(q_re, axis=0), jnp.sum(q_im, axis=0)], axis=0)
    return (patch_grads, probe_term)


def local(object_slices, probe_field, scan_offsets, scan_count, measured):
    layers, halves, tile_rows, tile_cols = object_slices.shape
    window = probe_field.shape[1]
    margin = window // 2
    slot_count = measured.shape[2]
    extended = with_halo(object_slices, (("row", 2), ("col", 3)), margin)
    row_starts = scan_offsets[0, 0, 0] - lax.axis_index("row") * tile_rows + margin
    col_starts = scan_offsets[0, 0, 1] - lax.axis_index("col") * tile_cols + margin
    live_mask = (jnp.arange(slot_count, dtype=jnp.int32) < scan_count[0, 0]).astype(jnp.float32)

    def take_patch(start_row, start_col):
        return lax.dynamic_slice(
            extended, (0, 0, start_row, start_col), (layers, halves, window, window)
        )

    patches = jax.vmap(take_patch)(row_starts, col_starts)
    patch_grads, probe_term = slot_gradients(patches, probe_field, measured[0, 0], live_mask)

    def place_slot(slot_index, accumulated):
        anchor = (0, 0, row_starts[slot_index], col_starts[slot_index])
        current = lax.dynamic_slice(accumulated, anchor, (layers, halves, window, window))
        return lax.dynamic_update_slice(accumulated, current + patch_grads[slot_index], anchor)

    start_grad = jnp.zeros((layers, halves, tile_rows + window, tile_cols + window), jnp.float32)
    extended_grad = lax.fori_loop(0, slot_count, place_slot, start_grad)
    down_sent = passed_along(extended_grad[:, :, tile_rows + margin :, :], "row", 1)
    up_sent = passed_along(extended_grad[:, :, :margin, :], "row", -1)
    middle_rows = extended_grad[:, :, margin : tile_rows + margin, :]
    middle_rows = middle_rows.at[:, :, :margin, :].add(down_sent)
    middle_rows = middle_rows.at[:, :, tile_rows - margin :, :].add(up_sent)
    right_sent = passed_along(middle_rows[:, :, :, tile_cols + margin :], "col", 1)
    left_sent = passed_along(middle_rows[:, :, :, :margin], "col", -1)
    object_grad = middle_rows[:, :, :, margin : tile_cols + margin]
    object_grad = object_grad.at[:, :, :, :margin].add(right_sent)
    object_grad = object_grad.at[:, :, :, tile_cols - margin :].add(left_sent)
    probe_total = lax.psum(probe_term, ("row", "col"))
    positions = lax.axis_size("row") * lax.axis_size("col") * slot_count
    probe_grad = probe_total / math.sqrt(positions)
    return (object_grad, probe_grad)


def solution(mesh):
    placed = (
        P(None, None, "row", "col"),
        P(),
        P("row", "col", None, None),
        P("row", "col"),
        P("row", "col", None, None, None),
    )
    return jax.shard_map(
        local,
        mesh=mesh,
        in_specs=placed,
        out_specs=(P(None, None, "row", "col"), P()),
        check_vma=False,
    )
```

profile of v0, /device:TPU:1, one launch (start us, length us, event | category | flops | bytes accessed | tf_op | source)
XLA Modules:
  0.0 617.1 jit_solution(11109015193168542818)
XLA Ops:
  8.6 4.1 collective-permute-start
  14.0 9.2 %collective-permute-done = f32[2,2,128,256]{3,2,1,0:T(8,128)S(1)} collective-permute-done((f32[2,2,128,256]{3,2,1,0:T(8,128)S(1)}, f32[2,2,128,256]{3,2,1,0:T(8,128)S(1)}, u32[]{:S(2)}, u32[]{:S(2)}) %collective-permute-start) | collective-permute-done | bytes 524320 | tf_op jit(solution)/shard_map/ppermute | solution.py:19
  23.5 3.6 collective-permute-done.1
  29.0 5.3 collective-permute-start.2
  40.9 11.0 %collective-permute-done.2 = f32[2,2,768,128]{3,2,1,0:T(8,128)} collective-permute-done((f32[2,2,768,128]{3,2,1,0:T(8,128)}, f32[2,2,768,128]{3,2,1,0:T(8,128)}, u32[]{:S(2)}, u32[]{:S(2)}) %collective-permute-start.2) | collective-permute-done | bytes 1572896 | tf_op jit(solution)/shard_map/ppermute | solution.py:19
  52.0 4.4 collective-permute-done.3
  56.4 5.2 pad_maximum_fusion
  61.6 18.9 %while.19 = (s32[]{:T(128)}, f32[2,2,768,512]{3,2,1,0:T(8,128)}, s32[4,4]{1,0:T(4,128)S(1)}, f32[4,2,2,256,256]{4,3,0,2,1:T(8,128)}, s32[]{:T(128)}) while((s32[]{:T(128)}, f32[2,2,768,512]{3,2,1,0:T(8,128)}, s32[4,4]{1,0:T(4,128)S(1)}, f32[4,2,2,256,256]{4,3,0,2,1:T(8,128)}, s32[]{:T(128)}) %tuple.83), condition=%wide.while_cond.4, body=%wide.while_body.4.sunk | while | flops 2 | bytes 2098301 | solution.py:123
  62.2 4.1 bitcast_dynamic-update-slice_fusion.2
  66.8 4.0 bitcast_dynamic-update-slice_fusion.2
  71.5 4.1 bitcast_dynamic-update-slice_fusion.2
  76.1 4.1 bitcast_dynamic-update-slice_fusion.2
  80.5 4.4 fusion.100
  85.0 4.3 fusion.104
  89.2 2.8 fusion.11
  94.8 3.2 fusion.102
  98.0 2.8 fusion.10
  106.3 2.9 fusion.93
  109.2 2.8 fusion.97
  112.0 2.8 fusion.9
  120.2 3.0 fusion.8
  126.0 3.0 fusion.16
  131.7 3.1 fusion.90
  137.4 2.7 fusion.56
  142.9 2.9 fusion.6
  148.6 3.1 fusion.26
  157.1 2.9 fusion.5
  168.1 3.1 convolution_add_fusion.4
  171.2 3.1 fusion.18
  179.7 2.8 fusion.3
  193.4 2.9 convolution_subtract_fusion.2
  196.3 2.8 fusion.67
  199.1 2.8 fusion.71
  201.8 2.8 fusion.1
  204.6 3.1 fusion.36
  210.5 2.8 fusion
  213.4 2.7 convolution_subtract_fusion
  216.2 3.5 fusion.22
  222.1 3.5 broadcast_in_dim.6
  225.6 76.6 %while.18 = (s32[]{:T(128)}, f32[2,2,768,512]{3,2,1,0:T(8,128)}, s32[4]{0:T(128)S(1)}, s32[4]{0:T(128)S(1)}, f32[4,2,2,256,256]{4,3,0,2,1:T(8,128)}, /*index=5*/s32[]{:T(128)}, s32[]{:T(128)}, s32[]{:T(128)}, s32[]{:T(128)}) while((s32[]{:T(128)}, f32[2,2,768,512]{3,2,1,0:T(8,128)}, s32[4]{0:T(128)S(1)}, s32[4]{0:T(128)S(1)}, ...), condition=%wide.region_1.2_spmd, body=%wide.region_0.1_spmd.sunk | while | flops 262152 | bytes 5243089 | solution.py:136
  232.8 11.9 %dynamic_update_slice.8 = f32[2,2,768,512]{3,2,1,0:T(8,128)} dynamic-update-slice(f32[2,2,768,512]{3,2,1,0:T(8,128)} %get-tuple-element.297, f32[2,2,256,256]{3,2,1,0:T(8,128)S(1)} %bitcast_add_fusion.2, s32[]{:T(128)} %constant.187.clone.1..sunk, s32[]{:T(128)} %constant.187.clone.1..sunk, s32[]{:T(128)S(6)} %select_n.348, s32[]{:T(128)S(6)} %select_n.349) | dynamic-update-slice | bytes 2097156 | tf_op jit(solution)/shard_map/while/body/eval_jaxpr/dynamic_update_slice | solution.py:133
  251.9 11.9 %dynamic_update_slice.8 = f32[2,2,768,512]{3,2,1,0:T(8,128)} dynamic-update-slice(f32[2,2,768,512]{3,2,1,0:T(8,128)} %get-tuple-element.297, f32[2,2,256,256]{3,2,1,0:T(8,128)S(1)} %bitcast_add_fusion.2, s32[]{:T(128)} %constant.187.clone.1..sunk, s32[]{:T(128)} %constant.187.clone.1..sunk, s32[]{:T(128)S(6)} %select_n.348, s32[]{:T(128)S(6)} %select_n.349) | dynamic-update-slice | bytes 2097156 | tf_op jit(solution)/shard_map/while/body/eval_jaxpr/dynamic_update_slice | solution.py:133
  270.9 12.3 %dynamic_update_slice.8 = f32[2,2,768,512]{3,2,1,0:T(8,128)} dynamic-update-slice(f32[2,2,768,512]{3,2,1,0:T(8,128)} %get-tuple-element.297, f32[2,2,256,256]{3,2,1,0:T(8,128)S(1)} %bitcast_add_fusion.2, s32[]{:T(128)} %constant.187.clone.1..sunk, s32[]{:T(128)} %constant.187.clone.1..sunk, s32[]{:T(128)S(6)} %select_n.348, s32[]{:T(128)S(6)} %select_n.349) | dynamic-update-slice | bytes 2097156 | tf_op jit(solution)/shard_map/while/body/eval_jaxpr/dynamic_update_slice | solution.py:133
  290.4 11.8 %dynamic_update_slice.8 = f32[2,2,768,512]{3,2,1,0:T(8,128)} dynamic-update-slice(f32[2,2,768,512]{3,2,1,0:T(8,128)} %get-tuple-element.297, f32[2,2,256,256]{3,2,1,0:T(8,128)S(1)} %bitcast_add_fusion.2, s32[]{:T(128)} %constant.187.clone.1..sunk, s32[]{:T(128)} %constant.187.clone.1..sunk, s32[]{:T(128)S(6)} %select_n.348, s32[]{:T(128)S(6)} %select_n.349) | dynamic-update-slice | bytes 2097156 | tf_op jit(solution)/shard_map/while/body/eval_jaxpr/dynamic_update_slice | solution.py:133
  304.0 4.2 collective-permute-start.4
  312.2 7.7 %collective-permute-done.4 = f32[2,2,128,512]{3,2,1,0:T(8,128)S(1)} collective-permute-done((f32[2,2,128,512]{3,2,1,0:T(8,128)S(1)}, f32[2,2,128,512]{3,2,1,0:T(8,128)S(1)}, u32[]{:S(2)}, u32[]{:S(2)}) %collective-permute-start.4) | collective-permute-done | bytes 1048608 | tf_op jit(solution)/shard_map/ppermute | solution.py:28
  327.7 10.9 %collective-permute-start.6 = (f32[2,2,512,128]{3,2,1,0:T(8,128)}, f32[2,2,512,128]{3,2,1,0:T(8,128)S(1)}, u32[]{:S(2)}, u32[]{:S(2)}) collective-permute-start(f32[2,2,512,128]{3,2,1,0:T(8,128)} %get-tuple-element.187), channel_id=1, source_target_pairs={{0,1},{1,2},{2,3},{3,4},{4,5},{5,6},{6,7},{7,8},{8,9},{9,10},{10,1... | collective-permute-start | bytes 3145736 | tf_op jit(solution)/shard_map/ppermute | solution.py:28
  341.4 262.1 %all-reduce.2.cloned.1.call-done = f32[2,256,256]{2,1,0:T(8,128)} async-done(((f32[2,256,256]{2,1,0:T(8,128)}), f32[2,256,256]{2,1,0:T(8,128)}) %all-reduce.2.cloned.1.call-update) | async-done | bytes 524304 | tf_op jit(solution)/shard_map/psum | solution.py:147
  (101 shorter events, 111.2 us)
Async XLA Ops:
  7.2 596.4 %all-reduce.2.cloned.1.call-start = ((), (), s32[]{:S(2)}) async-start(), calls=%async_computation | async-start | bytes 1048576 | tf_op jit(solution)/shard_map/psum | solution.py:147
  7.2 16.1 %copy-start.7 = (f32[2,2,512,256]{3,2,1,0:T(8,128)S(1)}, f32[2,2,512,256]{3,2,1,0:T(8,128)}, u32[]{:S(2)}) copy-start(f32[2,2,512,256]{3,2,1,0:T(8,128)} %param.15) | copy-start | bytes 6291460
  8.6 14.6 %collective-permute-start = (f32[2,2,128,256]{3,2,1,0:T(8,128)S(1)}, f32[2,2,128,256]{3,2,1,0:T(8,128)S(1)}, u32[]{:S(2)}, u32[]{:S(2)}) collective-permute-start(f32[2,2,128,256]{3,2,1,0:T(8,128)S(1)} %get-tuple-element.199), channel_id=1, source_target_pairs={{0,32},{32,64},{64,96},{96,128},{128,160},{160,192},{192,224},{1,3... | collective-permute-start | bytes 1572872 | tf_op jit(solution)/shard_map/ppermute | solution.py:19
  12.7 14.4 %collective-permute-start.1 = (f32[2,2,128,256]{3,2,1,0:T(8,128)S(1)}, f32[2,2,128,256]{3,2,1,0:T(8,128)S(1)}, u32[]{:S(2)}, u32[]{:S(2)}) collective-permute-start(f32[2,2,128,256]{3,2,1,0:T(8,128)S(1)} %get-tuple-element.198), channel_id=1, source_target_pairs={{32,0},{64,32},{96,64},{128,96},{160,128},{192,160},{224,192},{33,... | collective-permute-start | bytes 1572872 | tf_op jit(solution)/shard_map/ppermute | solution.py:20
  23.5 13.5 %copy-start.8 = (s32[1,1,2,4]{3,2,1,0:T(2,128)S(1)}, s32[1,1,2,4]{3,2,1,0:T(2,128)}, u32[]{:S(2)}) copy-start(s32[1,1,2,4]{3,2,1,0:T(2,128)} %param.17) | copy-start | bytes 100
  29.0 22.9 %collective-permute-start.2 = (f32[2,2,768,128]{3,2,1,0:T(8,128)}, f32[2,2,768,128]{3,2,1,0:T(8,128)}, u32[]{:S(2)}, u32[]{:S(2)}) collective-permute-start(f32[2,2,768,128]{3,2,1,0:T(8,128)} %get-tuple-element.190), channel_id=1, source_target_pairs={{0,1},{1,2},{2,3},{3,4},{4,5},{5,6},{6,7},{7,8},{8,9},{9,10},{10,1... | collective-permute-start | bytes 4718600 | tf_op jit(solution)/shard_map/ppermute | solution.py:19
  34.3 22.1 %collective-permute-start.3 = (f32[2,2,768,128]{3,2,1,0:T(8,128)}, f32[2,2,768,128]{3,2,1,0:T(8,128)}, u32[]{:S(2)}, u32[]{:S(2)}) collective-permute-start(f32[2,2,768,128]{3,2,1,0:T(8,128)} %get-tuple-element.191), channel_id=1, source_target_pairs={{1,0},{2,1},{3,2},{4,3},{5,4},{6,5},{7,6},{8,7},{9,8},{10,9},{11,1... | collective-permute-start | bytes 4718600 | tf_op jit(solution)/shard_map/ppermute | solution.py:20
  61.6 18.9 %copy-start.2 = (f32[256,256]{1,0:T(8,128)S(1)}, f32[256,256]{1,0:T(8,128)}, u32[]{:S(2)}) copy-start(f32[256,256]{1,0:T(8,128)} %get-tuple-element.200) | copy-start | bytes 786436
  61.6 18.9 %copy-start.3 = (f32[256,256]{1,0:T(8,128)S(1)}, f32[256,256]{1,0:T(8,128)}, u32[]{:S(2)}) copy-start(f32[256,256]{1,0:T(8,128)} %get-tuple-element.201) | copy-start | bytes 786436
  80.5 8.7 %copy-start.1 = (f32[4,2,2,256,256]{4,3,0,2,1:T(8,128)S(1)}, f32[4,2,2,256,256]{4,3,0,2,1:T(8,128)}, u32[]{:S(2)}) copy-start(f32[4,2,2,256,256]{4,3,0,2,1:T(8,128)} %get-tuple-element.152) | copy-start | bytes 12582916
  98.0 8.3 %copy-start.5 = (f32[256,256]{1,0:T(8,128)S(1)}, f32[256,256]{1,0:T(8,128)}, u32[]{:S(2)}) copy-start(f32[256,256]{1,0:T(8,128)} %get-tuple-element.204) | copy-start | bytes 786436
  140.2 8.3 %copy-start.9 = (f32[1,1,4,256,256]{4,3,2,1,0:T(8,128)S(1)}, f32[1,1,4,256,256]{4,3,2,1,0:T(8,128)}, u32[]{:S(2)}) copy-start(f32[1,1,4,256,256]{4,3,2,1,0:T(8,128)} %param.19) | copy-start | bytes 3145732
  188.0 8.3 %copy-start.4 = (f32[256,256]{1,0:T(8,128)S(1)}, f32[256,256]{1,0:T(8,128)}, u32[]{:S(2)}) copy-start(f32[256,256]{1,0:T(8,128)} %get-tuple-element.202) | copy-start | bytes 786436
  304.0 15.8 %collective-permute-start.4 = (f32[2,2,128,512]{3,2,1,0:T(8,128)S(1)}, f32[2,2,128,512]{3,2,1,0:T(8,128)S(1)}, u32[]{:S(2)}, u32[]{:S(2)}) collective-permute-start(f32[2,2,128,512]{3,2,1,0:T(8,128)S(1)} %get-tuple-element.181), channel_id=1, source_target_pairs={{0,32},{32,64},{64,96},{96,128},{128,160},{160,192},{192,224},{1,3... | collective-permute-start | bytes 3145736 | tf_op jit(solution)/shard_map/ppermute | solution.py:28
  308.2 15.8 %collective-permute-start.5 = (f32[2,2,128,512]{3,2,1,0:T(8,128)S(1)}, f32[2,2,128,512]{3,2,1,0:T(8,128)S(1)}, u32[]{:S(2)}, u32[]{:S(2)}) collective-permute-start(f32[2,2,128,512]{3,2,1,0:T(8,128)S(1)} %get-tuple-element.180), channel_id=1, source_target_pairs={{32,0},{64,32},{96,64},{128,96},{160,128},{192,160},{224,192},{33,... | collective-permute-start | bytes 3145736 | tf_op jit(solution)/shard_map/ppermute | solution.py:28
  324.3 2.0 copy-start
  327.7 279.4 %collective-permute-start.6 = (f32[2,2,512,128]{3,2,1,0:T(8,128)}, f32[2,2,512,128]{3,2,1,0:T(8,128)S(1)}, u32[]{:S(2)}, u32[]{:S(2)}) collective-permute-start(f32[2,2,512,128]{3,2,1,0:T(8,128)} %get-tuple-element.187), channel_id=1, source_target_pairs={{0,1},{1,2},{2,3},{3,4},{4,5},{5,6},{6,7},{7,8},{8,9},{9,10},{10,1... | collective-permute-start | bytes 3145736 | tf_op jit(solution)/shard_map/ppermute | solution.py:28
  338.6 269.8 %collective-permute-start.7 = (f32[2,2,512,128]{3,2,1,0:T(8,128)}, f32[2,2,512,128]{3,2,1,0:T(8,128)S(1)}, u32[]{:S(2)}, u32[]{:S(2)}) collective-permute-start(f32[2,2,512,128]{3,2,1,0:T(8,128)} %get-tuple-element.186), channel_id=1, source_target_pairs={{1,0},{2,1},{3,2},{4,3},{5,4},{6,5},{7,6},{8,7},{9,8},{10,9},{11,1... | collective-permute-start | bytes 3145736 | tf_op jit(solution)/shard_map/ppermute | solution.py:28
  608.7 1.3 copy-start.6
Sparse Core Ops, SparseCore 0:
  341.5 261.9 all-reduce.1
where the time goes:
time: 623 us; the launch traced here: 617 us
  waiting for transfers between devices  301 us (48%)
  matrix products  139 us (22%)
  local copies, waits for them, and re-layouts  91.2 us (15%)
  starting transfers between devices  30.9 us (5%)
  other arithmetic  24.2 us (4%)
  loops' own time  15.8 us (3%)
  between operations  15.6 us (3%)
    psum x1, waiting for transfers between devices, local(): probe_total = lax.psum(probe_term, ('row', 'col'))  262 us
    dynamic_update_slice x4, local copies, waits for them, and re-layouts, place_slot(): lax.dynamic_update_slice(accumulated, current + patch_grads[slot_index],...  47.8 us
    ppermute x2, waiting for transfers between devices, with_halo(): before = lax.ppermute(last, axis, up)  20.3 us
    gather x12, local copies, waits for them, and re-layouts  18.6 us
    ppermute x4, starting transfers between devices, passed_along(): return lax.ppermute(block, axis, route)  18.3 us
    dot_general x6, matrix products, transform(): jnp.einsum('jk,skl->sjl', c_re, x_re, precision=highest)  18.2 us
    dot_general x6, matrix products, transform(): jnp.einsum('jk,skl->sjl', c_re, x_im, precision=highest)  18.1 us
    dot_general x6, matrix products, transform(): jnp.einsum('sjk,kl->sjl', y_im, c_re, precision=highest)  17.9 us
  transfers between devices with their start and end apart: 9, of which 7 were waited for; matrix products, arithmetic and copies ran while one was open for 2% of the time, Pallas kernels for 0%

commit v1 on v0

v1 whole, which is shorter than its diff:
```python
import functools
import math

import jax
import jax.numpy as jnp
import ml_dtypes
import numpy as np
from jax import lax
from jax.experimental import pallas as pl
from jax.experimental.pallas import tpu as pltpu
from jax.sharding import PartitionSpec as P

DEFOCUS = 0.3
FLOOR = 0.5


def real_form(m):
    return np.block([[m.real, -m.imag], [m.imag, m.real]])


def stage_matrices(window):
    half = window // 2
    index = np.arange(window)
    dft = np.exp(-2j * np.pi * (index[:, None] * index[None, :] % window) / window) / math.sqrt(window)
    freq = (index + half) % window - half
    phase = np.exp(-1j * np.pi * DEFOCUS * freq**2 / window)
    spread = dft.conj() @ (phase[:, None] * dft)
    near, far = spread[:half, :half], spread[:half, half:]
    parts = []
    for m in ((near + far) / 2, (near - far) / 2, dft[0::2, :half], dft[1::2, :half]):
        form = real_form(m)
        parts += [form, form.T]
    stack = []
    for form in parts:
        form = form.astype(np.float32)
        high = form.astype(ml_dtypes.bfloat16)
        low = (form - high.astype(np.float32)).astype(ml_dtypes.bfloat16)
        stack.append(np.concatenate([high, low], axis=1))
    return np.stack(stack)


PU, PU_T, PV, PV_T, FE, FE_T, FO, FO_T = range(8)


def split(x):
    high = x.astype(jnp.bfloat16)
    low = (x - high.astype(jnp.float32)).astype(jnp.bfloat16)
    return high, low


def dot(a, b):
    return jnp.dot(a, b, preferred_element_type=jnp.float32)


def from_left(w_ref, which, x):
    n = x.shape[0]
    high, low = split(x)
    wh, wl = w_ref[which, :, :n], w_ref[which, :, n:]
    return dot(wh, high) + dot(wh, low) + dot(wl, high)


def from_right(w_ref, which, x):
    n = x.shape[1]
    high, low = split(x)
    wh, wl = w_ref[which, :, :n], w_ref[which, :, n:]
    return dot(high, wh) + dot(low, wh) + dot(high, wl)


def rows(*parts):
    return jnp.concatenate(parts, axis=0)


def lanes(*parts):
    return jnp.concatenate(parts, axis=1)


def spread_field(w_ref, mats, xr, xi):
    u, v, ut, vt = mats
    h = xr.shape[0] // 2
    a = from_left(w_ref, u, rows(xr[:h] + xr[h:], xi[:h] + xi[h:]))
    b = from_left(w_ref, v, rows(xr[:h] - xr[h:], xi[:h] - xi[h:]))
    p, m = a + b, a - b
    yr, yi = rows(p[:h], m[:h]), rows(p[h:], m[h:])
    a = from_right(w_ref, ut, lanes(yr[:, :h] + yr[:, h:], yi[:, :h] + yi[:, h:]))
    b = from_right(w_ref, vt, lanes(yr[:, :h] - yr[:, h:], yi[:, :h] - yi[:, h:]))
    p, m = a + b, a - b
    return lanes(p[:, :h], m[:, :h]), lanes(p[:, h:], m[:, h:])


def to_far(w_ref, xr, xi):
    h = xr.shape[0] // 2
    e = from_left(w_ref, FE, rows(xr[:h] + xr[h:], xi[:h] + xi[h:]))
    o = from_left(w_ref, FO, rows(xr[:h] - xr[h:], xi[:h] - xi[h:]))
    yr, yi = rows(e[:h], o[:h]), rows(e[h:], o[h:])
    qe = from_right(w_ref, FE_T, lanes(yr[:, :h] + yr[:, h:], yi[:, :h] + yi[:, h:]))
    qo = from_right(w_ref, FO_T, lanes(yr[:, :h] - yr[:, h:], yi[:, :h] - yi[:, h:]))
    return qe, qo


def from_far(w_ref, ge, go):
    h = ge.shape[0] // 2
    a = from_right(w_ref, FE, ge)
    b = from_right(w_ref, FO, go)
    p, m = a + b, a - b
    yr, yi = lanes(p[:, :h], m[:, :h]), lanes(p[:, h:], m[:, h:])
    a = from_left(w_ref, FE_T, rows(yr[:h], yi[:h]))
    b = from_left(w_ref, FO_T, rows(yr[h:], yi[h:]))
    p, m = a + b, a - b
    return rows(p[:h], m[:h]), rows(p[h:], m[h:])


def window_kernel(rs_ref, cs_ref, count_ref, ext_ref, probe_ref, meas_ref, w_ref,
                  gext_ref, pg_ref, t_ref, psi_ref, m_ref):
    slots, n = meas_ref.shape[0], meas_ref.shape[1]
    h = n // 2
    gext_ref[...] = jnp.zeros_like(gext_ref)
    pg_ref[...] = jnp.zeros_like(pg_ref)
    lane = lax.broadcasted_iota(jnp.int32, (n + 8, h), 1)
    sub = lax.broadcasted_iota(jnp.int32, (n // 8, 8, h), 1)
    wide = lax.broadcasted_iota(jnp.int32, (n // 8 + 1, 8, h), 1)
    pick = lax.rem(lane[:n], h // 2) * 2
    first = lane[:n] < h // 2

    @pl.loop(0, slots)
    def _(s):
        r = rs_ref[s]
        c = cs_ref[s]
        base = lax.div(c, h)
        shift = c - base * h
        back = lax.rem(h - shift, h)
        top = pl.multiple_of(lax.div(r, 8) * 8, 8)
        down = r - top
        up = lax.rem(8 - down, 8)
        tall = n + 8
        for layer in range(2):
            for part in range(2):
                raw = [ext_ref[base + k, layer, part, pl.ds(top, tall), :] for k in range(3)]
                raw = [pltpu.roll(x, back, 1) for x in raw]
                for k in range(2):
                    x = jnp.where(lane < h - shift, raw[k], raw[k + 1])
                    x = pltpu.roll(x.reshape(tall // 8, 8, h), up, 1)
                    x = jnp.where(sub < 8 - down, x[:-1], x[1:])
                    t_ref[layer, part, :, k * h : (k + 1) * h] = x.reshape(n, h)
        pr, pi = probe_ref[0], probe_ref[1]
        tr, ti = t_ref[0, 0], t_ref[0, 1]
        xr, xi = spread_field(w_ref, (PU, PV, PU_T, PV_T), tr * pr - ti * pi, tr * pi + ti * pr)
        psi_ref[0] = xr
        psi_ref[1] = xi
        tr, ti = t_ref[1, 0], t_ref[1, 1]
        qe, qo = to_far(w_ref, tr * xr - ti * xi, tr * xi + ti * xr)
        live = jnp.where(s < count_ref[0], 1.0, 0.0).astype(jnp.float32)

        for par in range(2):
            got = [jnp.take_along_axis(meas_ref[s, :, k * h : (k + 1) * h], pick + par, axis=1) for k in range(2)]
            m_ref[par] = jnp.where(first, got[0], got[1])

        g = []
        for par, q in ((0, qe), (1, qo)):
            fr, fi = q[:, :h], q[:, h:]
            inv = lax.rsqrt(jnp.maximum(fr * fr + fi * fi, FLOOR * FLOOR))
            weight = live * (1.0 - rows(*[m_ref[par, pl.ds(rp, h, stride=2), :] for rp in range(2)]) * inv)
            g.append(lanes(weight * fr, weight * fi))
        br, bi = from_far(w_ref, *g)

        def place(layer, gr, gi):
            for part, x in ((0, gr), (1, gi)):
                moved = []
                for k in range(2):
                    y = pltpu.roll(x[:, k * h : (k + 1) * h].reshape(n // 8, 8, h), down, 1)
                    zero = jnp.zeros((1, 8, h), jnp.float32)
                    y = jnp.where(wide < down, rows(zero, y), rows(y, zero))
                    moved.append(pltpu.roll(y.reshape(tall, h), shift, 1))
                a, b = moved
                low = lane < shift
                zero = jnp.zeros_like(a)
                pieces = (jnp.where(low, zero, a), jnp.where(low, a, b), jnp.where(low, b, zero))
                for k, piece in enumerate(pieces):
                    where = (base + k, layer, part, pl.ds(top, tall), slice(None))
                    gext_ref[where] = gext_ref[where] + piece

        xr, xi = psi_ref[0], psi_ref[1]
        place(1, xr * br + xi * bi, xr * bi - xi * br)
        tr, ti = t_ref[1, 0], t_ref[1, 1]
        br, bi = spread_field(w_ref, (PU_T, PV_T, PU, PV), tr * br + ti * bi, tr * bi - ti * br)
        pr, pi = probe_ref[0], probe_ref[1]
        place(0, pr * br + pi * bi, pr * bi - pi * br)
        tr, ti = t_ref[0, 0], t_ref[0, 1]
        for part, x in ((0, tr * br + ti * bi), (1, tr * bi - ti * br)):
            for k in range(2):
                pg_ref[part * 2 + k] += x[:, k * h : (k + 1) * h]


def windows(rs, cs, count, ext, probe, meas, w):
    vmem = pl.BlockSpec(memory_space=pltpu.VMEM)
    smem = pl.BlockSpec(memory_space=pltpu.SMEM)
    n = probe.shape[1]
    return pl.pallas_call(
        window_kernel,
        out_shape=(jax.ShapeDtypeStruct(ext.shape, jnp.float32), jax.ShapeDtypeStruct((4, n, n // 2), jnp.float32)),
        in_specs=[smem, smem, smem, vmem, vmem, vmem, vmem],
        out_specs=(vmem, vmem),
        scratch_shapes=[pltpu.VMEM((2, 2, n, n), jnp.float32), pltpu.VMEM((2, n, n), jnp.float32),
                        pltpu.VMEM((2, n, n // 2), jnp.float32)],
        compiler_params=pltpu.CompilerParams(vmem_limit_bytes=48 << 20),
        name="windows",
    )(rs, cs, count, ext, probe, meas, w)


MESH = pl.DeviceIdType.MESH


def remote(src, dst, send, recv, target):
    return pltpu.make_async_remote_copy(
        src_ref=src, dst_ref=dst, send_sem=send, recv_sem=recv, device_id=target, device_id_type=MESH
    )


def greet(peers):
    barrier = pltpu.get_barrier_semaphore()
    total = 0
    for there, target in peers:
        @pl.when(there)
        def _(target=target):
            pl.semaphore_signal(barrier, inc=1, device_id=target, device_id_type=MESH)
        total = total + jnp.where(there, 1, 0)
    pl.semaphore_wait(barrier, total)


def neighbours():
    row, col = lax.axis_index("row"), lax.axis_index("col")
    n_row, n_col = lax.axis_size("row"), lax.axis_size("col")
    return {
        "up": (row > 0, {"row": row - 1, "col": col}),
        "down": (row < n_row - 1, {"row": row + 1, "col": col}),
        "left": (col > 0, {"row": row, "col": col - 1}),
        "right": (col < n_col - 1, {"row": row, "col": col + 1}),
    }


OPPOSITE = {"up": "down", "down": "up", "left": "right", "right": "left"}
SIDES = ("up", "down", "left", "right")


def halo_kernel(obj_ref, ext_ref, local_sem, send_sem, recv_sem):
    rows_, h = obj_ref.shape[2], ext_ref.shape[4]
    near = neighbours()
    top = slice(0, h), slice(0, h)
    greet([near[side] for side in SIDES])
    own = [pltpu.make_async_copy(obj_ref.at[:, :, :, pl.ds(b * h, h)], ext_ref.at[1 + b, :, :, pl.ds(h, rows_), :], local_sem.at[b]) for b in range(2)]
    first = []
    for layer in range(2):
        first.append((0 + layer, "right", obj_ref.at[layer, :, :, pl.ds(h, h)], ext_ref.at[0, layer, :, pl.ds(h, rows_), :]))
        first.append((2 + layer, "left", obj_ref.at[layer, :, :, pl.ds(0, h)], ext_ref.at[3, layer, :, pl.ds(h, rows_), :]))
        for b in range(2):
            first.append((4 + layer * 2 + b, "down", obj_ref.at[layer, :, pl.ds(rows_ - h, h), pl.ds(b * h, h)], ext_ref.at[1 + b, layer, :, pl.ds(0, h), :]))
            first.append((8 + layer * 2 + b, "up", obj_ref.at[layer, :, pl.ds(0, h), pl.ds(b * h, h)], ext_ref.at[1 + b, layer, :, pl.ds(rows_ + h, h), :]))
    copies = {}
    for number, side, src, dst in first:
        copies[number] = (side, remote(src, dst, send_sem.at[number], recv_sem.at[number], near[side][1]))
    for number in sorted(copies, key=lambda i: (i % 2 if i < 4 else (i - 4) // 2 % 2, i)):
        side, copy = copies[number]
        pl.when(near[side][0])(copy.start)
    for copy in own:
        copy.start()
    for layer in range(2):
        for b in range(2):
            side = ("left", "right")[b]
            for k, (source_side, start) in enumerate((("up", 0), ("down", rows_ + h))):
                came = (4, 8)[k] + layer * 2 + b
                number = 12 + layer * 4 + b * 2 + k
                block = ext_ref.at[1 + b, layer, :, pl.ds(start, h), :]
                copy = remote(block, ext_ref.at[(3, 0)[b], layer, :, pl.ds(start, h), :], send_sem.at[number], recv_sem.at[number], near[side][1])
                copies[number] = (side, copy)

                @pl.when(near[source_side][0])
                def _(came=came, side=side, copy=copy):
                    copies[came][1].wait_recv()
                    pl.when(near[side][0])(copy.start)
    for number, (side, copy) in copies.items():
        vertical = 4 <= number < 12
        corner = number >= 12
        source_side = ("up", "down")[number % 2] if corner else None

        def finish(copy=copy, side=side, vertical=vertical):
            pl.when(near[side][0])(copy.wait_send)
            if not vertical:
                pl.when(near[OPPOSITE[side]][0])(copy.wait_recv)

        if corner:
            pl.when(near[source_side][0])(finish)
        else:
            finish()
    for copy in own:
        copy.wait()


def halo(obj):
    layers, parts, rows_, cols = obj.shape
    h = cols // 2
    return pl.pallas_call(
        halo_kernel,
        out_shape=jax.ShapeDtypeStruct((4, layers, parts, rows_ + 2 * h, h), jnp.float32),
        in_specs=[pl.BlockSpec(memory_space=pl.ANY)],
        out_specs=pl.BlockSpec(memory_space=pltpu.VMEM),
        scratch_shapes=[pltpu.SemaphoreType.DMA((2,)), pltpu.SemaphoreType.DMA((20,)), pltpu.SemaphoreType.DMA((20,))],
        compiler_params=pltpu.CompilerParams(collective_id=0, has_side_effects=True, vmem_limit_bytes=16 << 20),
        name="halo",
    )(obj)


def back_kernel(gext_ref, pg_ref, side_ref, strip_ref, probe_ref,
                corner_ref, out_strip_ref, twin_ref, ring_ref, ring_sum_ref, group_ref, group_sum_ref,
                send_sem, recv_sem, group_send, group_recv, gather_send, gather_recv):
    h = gext_ref.shape[4]
    rows_ = gext_ref.shape[3] - 2 * h
    near = neighbours()
    row, col = lax.axis_index("row"), lax.axis_index("col")
    y, x_hi = lax.rem(row, 4), lax.div(row, 4)
    core, z, x_lo = lax.rem(col, 2), lax.rem(lax.div(col, 2), 8), lax.div(col, 16)
    group = x_hi * 16 + x_lo * 8 + z
    twin = {"row": row, "col": col + 1 - 2 * core}

    def ring_peer(k):
        return {"row": x_hi * 4 + lax.rem(y + k, 4), "col": col}

    def group_peer(k):
        g = lax.rem(group + k, 32)
        return {"row": lax.div(g, 16) * 4 + y, "col": lax.rem(g, 16) * 2 + core}, lax.rem(g, 16)

    def gather_peer(k):
        g = lax.rem(lax.rem(group, 16) + k, 16)
        return {"row": row, "col": g * 2 + core}

    barrier = pltpu.get_barrier_semaphore()
    total = 1 + 3 + 31
    for side in SIDES:
        there, target = near[side]

        @pl.when(there)
        def _(target=target):
            pl.semaphore_signal(barrier, inc=1, device_id=target, device_id_type=MESH)
        total = total + jnp.where(there, 1, 0)
    pl.semaphore_signal(barrier, inc=1, device_id=twin, device_id_type=MESH)
    for k in range(1, 4):
        pl.semaphore_signal(barrier, inc=1, device_id=ring_peer(k), device_id_type=MESH)

    @pl.loop(1, 32)
    def _(k):
        pl.semaphore_signal(barrier, inc=1, device_id=group_peer(k)[0], device_id_type=MESH)
    pl.semaphore_wait(barrier, total)

    def copy(number, src, dst, target):
        return remote(src, dst, send_sem.at[number], recv_sem.at[number], target)

    def at(start):
        return pl.ds(start, h)

    lows = (0, rows_ + h)
    corners = {}
    for b, side in enumerate(("left", "right")):
        for k in range(2):
            corners[b, k] = copy(b * 2 + k, gext_ref.at[b * 3, :, :, at(lows[k]), :], corner_ref.at[b, k], near[side][1])
            pl.when(near[side][0])(corners[b, k].start)
    twin_copy = copy(10, pg_ref.at[1 - core], twin_ref, twin)
    twin_copy.start()
    sides = {}
    for b, side in enumerate(("left", "right")):
        sides[b] = copy(4 + b, gext_ref.at[b * 3, :, :, pl.ds(h, rows_), :], side_ref.at[b], near[side][1])
        pl.when(near[side][0])(sides[b].start)

    strips = {}
    for k, side in enumerate(("up", "down")):
        for b in range(2):
            out_strip_ref[k, b] = gext_ref[1 + b, :, :, at(lows[k]), :]
            source = ("left", "right")[b]

            @pl.when(near[source][0])
            def _(k=k, b=b):
                corners[1 - b, k].wait_recv()
                out_strip_ref[k, b] += corner_ref[1 - b, k]
            strips[k, b] = copy(6 + k * 2 + b, out_strip_ref.at[k, b], strip_ref.at[k, b], near[side][1])
            pl.when(near[side][0])(strips[k, b].start)

    twin_copy.wait_recv()
    ring_ref[0] = pg_ref[core] + twin_ref[...]
    rings = []
    for k in range(1, 4):
        rings.append(copy(10 + k, ring_ref.at[0, lax.rem(y + k, 4)], ring_ref.at[k, 0], ring_peer(k)))
        rings[-1].start()
    for r in rings:
        r.wait_recv()
    ring_sum_ref[...] = ring_ref[0, y] + ring_ref[1, 0] + ring_ref[2, 0] + ring_ref[3, 0]

    def group_copy(k):
        target, piece = group_peer(k)
        return remote(ring_sum_ref.at[piece], group_ref.at[k], group_send.at[k], group_recv.at[k], target)

    @pl.loop(1, 32)
    def _(k):
        group_copy(k).start()
    mine = lax.rem(group, 16)
    group_ref[0] = ring_sum_ref[mine]

    @pl.loop(1, 32)
    def _(k):
        group_copy(k).wait_recv()
    group_sum_ref[mine] = jnp.sum(group_ref[...], axis=0)

    def gather_copy(k):
        return remote(group_sum_ref.at[mine], group_sum_ref.at[mine], gather_send.at[k], gather_recv.at[k], gather_peer(k))

    @pl.loop(1, 16)
    def _(k):
        gather_copy(k).start()

    @pl.loop(1, 16)
    def _(k):
        gather_copy(k).wait_recv()
    probe_ref[core, y] = group_sum_ref[...]
    gathers = []
    for k in range(1, 4):
        gathers.append(copy(13 + k, group_sum_ref, probe_ref.at[core, y], ring_peer(k)))
        gathers[-1].start()
    for g in gathers:
        g.wait_recv()
    last = copy(17, probe_ref.at[core], probe_ref.at[core], twin)
    last.start()
    last.wait_recv()

    for b, side in enumerate(("left", "right")):
        for k in range(2):
            pl.when(near[side][0])(corners[b, k].wait_send)
        pl.when(near[side][0])(sides[b].wait_send)
        pl.when(near[OPPOSITE[side]][0])(sides[b].wait_recv)
    for k, side in enumerate(("up", "down")):
        for b in range(2):
            pl.when(near[side][0])(strips[k, b].wait_send)
            pl.when(near[OPPOSITE[side]][0])(strips[k, b].wait_recv)
    twin_copy.wait_send()
    for c in rings + gathers + [last]:
        c.wait_send()

    @pl.loop(1, 32)
    def _(k):
        group_copy(k).wait_send()

    @pl.loop(1, 16)
    def _(k):
        gather_copy(k).wait_send()


def back(gext, pg):
    _, layers, parts, tall, h = gext.shape
    rows_ = tall - 2 * h
    vmem = pl.BlockSpec(memory_space=pltpu.VMEM)
    f32 = jnp.float32
    return pl.pallas_call(
        back_kernel,
        out_shape=(
            jax.ShapeDtypeStruct((2, layers, parts, rows_, h), f32),
            jax.ShapeDtypeStruct((2, 2, layers, parts, h, h), f32),
            jax.ShapeDtypeStruct((2, 4, 16, 8, 128), f32),
        ),
        in_specs=[vmem, vmem],
        out_specs=(vmem, vmem, vmem),
        scratch_shapes=[
            pltpu.VMEM((2, 2, layers, parts, h, h), f32),
            pltpu.VMEM((2, 2, layers, parts, h, h), f32),
            pltpu.VMEM((4, 16, 8, 128), f32),
            pltpu.VMEM((4, 4, 16, 8, 128), f32),
            pltpu.VMEM((16, 8, 128), f32),
            pltpu.VMEM((32, 8, 128), f32),
            pltpu.VMEM((16, 8, 128), f32),
            pltpu.SemaphoreType.DMA((18,)),
            pltpu.SemaphoreType.DMA((18,)),
            pltpu.SemaphoreType.DMA((32,)),
            pltpu.SemaphoreType.DMA((32,)),
            pltpu.SemaphoreType.DMA((16,)),
            pltpu.SemaphoreType.DMA((16,)),
        ],
        compiler_params=pltpu.CompilerParams(collective_id=1, has_side_effects=True, vmem_limit_bytes=32 << 20),
        name="back",
    )(gext, pg)


def join_kernel(n_row, n_col, place_ref, gext_ref, side_ref, strip_ref, out_ref):
    row, col = place_ref[0], place_ref[1]
    h = gext_ref.shape[4]
    rows_ = gext_ref.shape[3] - 2 * h
    for b in range(2):
        where = pl.ds(b * h, h)
        out_ref[:, :, :, where] = gext_ref[1 + b, :, :, pl.ds(h, rows_), :]

        @pl.when(col < n_col - 1 if b == 1 else col > 0)
        def _():
            out_ref[:, :, :, where] += side_ref[1 - b]

        @pl.when(row < n_row - 1)
        def _():
            out_ref[:, :, pl.ds(rows_ - h, h), where] += strip_ref[0, b]

        @pl.when(row > 0)
        def _():
            out_ref[:, :, pl.ds(0, h), where] += strip_ref[1, b]


def join(place, gext, side, strip):
    _, layers, parts, tall, h = gext.shape
    vmem = pl.BlockSpec(memory_space=pltpu.VMEM)
    return pl.pallas_call(
        functools.partial(join_kernel, lax.axis_size("row"), lax.axis_size("col")),
        out_shape=jax.ShapeDtypeStruct((layers, parts, tall - 2 * h, 2 * h), jnp.float32),
        in_specs=[pl.BlockSpec(memory_space=pltpu.SMEM), vmem, vmem, vmem],
        out_specs=vmem,
        compiler_params=pltpu.CompilerParams(vmem_limit_bytes=32 << 20),
        name="join",
    )(place, gext, side, strip)


def local(w, object_slices, probe_field, scan_offsets, scan_count, measured):
    layers, parts, tile_rows, tile_cols = object_slices.shape
    n = probe_field.shape[1]
    row, col = lax.axis_index("row"), lax.axis_index("col")
    ext = halo(object_slices)
    rs = scan_offsets[0, 0, 0] - row * tile_rows + n // 2
    cs = scan_offsets[0, 0, 1] - col * tile_cols + n // 2
    gext, pg = windows(rs, cs, scan_count[0], ext, probe_field, measured[0, 0], w)
    side, strip, total = back(gext, pg.reshape(2, 4, 16, 8, 128))
    object_grad = join(jnp.stack([row, col]).astype(jnp.int32), gext, side, strip)
    positions = lax.axis_size("row") * lax.axis_size("col") * measured.shape[2]
    probe_grad = total.reshape(2, 2, n, n // 2).transpose(0, 2, 1, 3).reshape(2, n, n) / math.sqrt(positions)
    return object_grad, probe_grad


def solution(mesh):
    placed = (
        P(None, None, "row", "col"),
        P(),
        P("row", "col", None, None),
        P("row", "col"),
        P("row", "col", None, None, None),
    )
    w = stage_matrices(256)
    return jax.shard_map(
        lambda *args: local(jnp.asarray(w), *args),
        mesh=mesh,
        in_specs=placed,
        out_specs=(P(None, None, "row", "col"), P()),
        check_vma=False,
    )
```

time: 623 us -> 122 us (0.20)
  waiting for transfers between devices: 301 us -> 0 us
  matrix products: 139 us -> 0 us
  Pallas kernels: 0 us -> 112 us
  local copies, waits for them, and re-layouts: 91.2 us -> 7.88 us
  starting transfers between devices: 30.9 us -> 0 us
  other arithmetic: 24.2 us -> 0.87 us
  loops' own time: 15.8 us -> 0 us
  between operations: 15.6 us -> 1.32 us
    psum x1 -> x0, waiting for transfers between devices: 262 us -> none  [local(): probe_total = lax.psum(probe_term, ('row', 'col'))]
    dot_general x48 -> x0, matrix products: 139 us -> none  [the longest x6 18.2 us: transform(): jnp.einsum('jk,skl->sjl', c_re, x_re, precision=highest)]
    pallas_call x0 -> x4, Pallas kernels: none -> 112 us  [the longest x1 68.9 us: back(): pl.pallas_call(back_kernel, out_shape=(jax.ShapeDtypeStruct((2, layers, p...]
    dynamic_update_slice x4 -> x0, local copies, waits for them, and re-layouts: 47.8 us -> none  [place_slot(): lax.dynamic_update_slice(accumulated, current + patch_grads[slot_index],...]
    ppermute x8 -> x0, waiting for transfers between devices: 38.7 us -> none  [the longest x2 20.3 us: with_halo(): before = lax.ppermute(last, axis, up)]
    ppermute x8 -> x0, starting transfers between devices: 30.8 us -> none  [the longest x4 18.3 us: passed_along(): return lax.ppermute(block, axis, route)]
    gather x12 -> x0, local copies, waits for them, and re-layouts: 18.6 us -> none
    another operation x2 -> x0, loops' own time: 15.8 us -> none  [the longest x1 15.6 us: local(): extended_grad = lax.fori_loop(0, slot_count, place_slot, start_grad)]
  transfers between devices with their start and end apart: 9 -> 0, of which waited for: 7 -> 0; matrix products, arithmetic and copies ran while one was open for 2% -> 0% of each run, Pallas kernels for 0% -> 0%
where the time goes in v1:
time: 122 us
  Pallas kernels  112 us (92%)
  local copies, waits for them, and re-layouts  7.88 us (6%)
  between operations  1.32 us (1%)
    pallas_call x1, Pallas kernels, back(): pl.pallas_call(back_kernel, out_shape=(jax.ShapeDtypeStruct((2, layers, p...  68.9 us
    pallas_call x1, Pallas kernels, halo(): pl.pallas_call(halo_kernel, out_shape=jax.ShapeDtypeStruct((4, layers, pa...  20.3 us
    pallas_call x1, Pallas kernels, windows(): pl.pallas_call(window_kernel, out_shape=(jax.ShapeDtypeStruct(ext.shape,...  20.2 us
    unnamed x12, local copies, waits for them, and re-layouts  7.05 us

profile of v1, /device:TPU:1, one launch (start us, length us, event | category | flops | bytes accessed | tf_op | source)
XLA Modules:
  0.0 121.7 jit_solution(6732019283538068331)
XLA Ops:
  1.3 0.1 pad_add_fusion.place_ref
  1.4 0.8 add_bitcast_fusion
  2.1 0.0 copy-start.2
  2.1 1.6 %copy-done.2 = f32[2,2,512,256]{3,2,1,0:T(8,128)S(1)} copy-done((f32[2,2,512,256]{3,2,1,0:T(8,128)S(1)}, f32[2,2,512,256]{3,2,1,0:T(8,128)}, u32[]{:S(2)}) %copy-start.2) | copy-done | bytes 2097176
  3.7 0.0 copy-start.3
  3.7 0.0 copy-start.4
  3.7 0.0 copy-start.5
  3.7 20.3 %halo.1.ext_ref = f32[4,2,2,768,128]{4,3,2,1,0:T(8,128)S(1)} custom-call(f32[2,2,512,256]{3,2,1,0:T(8,128)S(1)} %copy-done.2), custom_call_target="tpu_custom_call" | custom-call | tf_op jit(solution)/shard_map/halo/pallas_call | solution.py:300
  24.0 0.0 copy-start.1
  24.0 2.7 %copy-done.1 = f32[4,2,2,768,128]{4,3,2,1,0:T(8,128)} copy-done((f32[4,2,2,768,128]{4,3,2,1,0:T(8,128)}, f32[4,2,2,768,128]{4,3,2,1,0:T(8,128)S(1)}, u32[]{:S(2)}) %copy-start.1) | copy-done | bytes 6291480
  26.7 0.0 copy-done.3
  26.7 0.0 copy-done.4
  26.7 0.0 copy-done.5
  26.7 20.2 %windows.1 = (f32[4,2,2,768,128]{4,3,2,1,0:T(8,128)}, f32[4,256,128]{2,1,0:T(8,128)S(1)}) custom-call(s32[4]{0:T(128)S(1)} %get-tuple-element.13.rs_ref, s32[4]{0:T(128)S(1)} %get-tuple-element.12.cs_ref, s32[1]{0:T(128)} %bitcast.19.count_ref, f32[4,2,2,768,128]{4,3,2,1,0:T(8,128)} %copy-done.1, f32[2,256,256]{2,1,0:T(8,128)S(1)} %copy-done.5, ...), custom_call_target="tpu_custom_call" | custom-call | tf_op jit(solution)/shard_map/windows/pallas_call | solution.py:197
  46.9 0.0 copy-start
  46.9 2.8 %copy-done = f32[4,2,2,768,128]{4,3,2,1,0:T(8,128)S(1)} copy-done((f32[4,2,2,768,128]{4,3,2,1,0:T(8,128)S(1)}, f32[4,2,2,768,128]{4,3,2,1,0:T(8,128)}, u32[]{:S(2)}) %copy-start) | copy-done | bytes 6291480
  49.7 68.9 %back.1 = (f32[2,2,2,512,128]{4,3,2,1,0:T(8,128)S(1)}, f32[2,2,2,2,128,128]{5,4,3,2,1,0:T(8,128)S(1)}, f32[2,4,16,8,128]{4,3,2,1,0:T(8,128)S(1)}) custom-call(f32[4,2,2,768,128]{4,3,2,1,0:T(8,128)S(1)} %copy-done, f32[2,4,16,8,128]{4,3,2,1,0:T(8,128)S(1)} %bitcast.21), custom_call_target="tpu_custom_call" | custom-call | tf_op jit(solution)/shard_map/back/pallas_call | solution.py:457
  118.5 2.3 %join.1 = f32[2,2,512,256]{3,2,1,0:T(8,128)} custom-call(s32[2]{0:T(128)S(1)} %pad_add_fusion.place_ref, f32[4,2,2,768,128]{4,3,2,1,0:T(8,128)S(1)} %copy-done, f32[2,2,2,512,128]{4,3,2,1,0:T(8,128)S(1)} %get-tuple-element.9.side_ref, f32[2,2,2,2,128,128]{5,4,3,2,1,0:T(8,128)S(1)} %get-tuple-element.10.strip_ref), custom_call_target="tpu_custom_call" | custom-call | tf_op jit(solution)/shard_map/join/pallas_call | solution.py:510
  120.9 0.8 copy_bitcast_fusion
  (1 shorter events, 0.0 us)
Async XLA Ops:
  2.1 1.6 %copy-start.2 = (f32[2,2,512,256]{3,2,1,0:T(8,128)S(1)}, f32[2,2,512,256]{3,2,1,0:T(8,128)}, u32[]{:S(2)}) copy-start(f32[2,2,512,256]{3,2,1,0:T(8,128)} %obj_ref.1) | copy-start | bytes 6291460
  3.7 23.0 %copy-start.3 = (bf16[8,256,512]{2,1,0:T(8,128)(2,1)S(1)}, bf16[8,256,512]{2,1,0:T(8,128)(2,1)}, u32[]{:S(2)}) copy-start(bf16[8,256,512]{2,1,0:T(8,128)(2,1)} %constant.20.clone.w_ref) | copy-start | bytes 6291460
  3.7 23.0 %copy-start.4 = (f32[1,1,4,256,256]{4,3,2,1,0:T(8,128)S(1)}, f32[1,1,4,256,256]{4,3,2,1,0:T(8,128)}, u32[]{:S(2)}) copy-start(f32[1,1,4,256,256]{4,3,2,1,0:T(8,128)} %param.10) | copy-start | bytes 3145732
  3.7 23.0 %copy-start.5 = (f32[2,256,256]{2,1,0:T(8,128)S(1)}, f32[2,256,256]{2,1,0:T(8,128)}, u32[]{:S(2)}) copy-start(f32[2,256,256]{2,1,0:T(8,128)} %probe_ref.1) | copy-start | bytes 1572868
  24.0 2.7 %copy-start.1 = (f32[4,2,2,768,128]{4,3,2,1,0:T(8,128)}, f32[4,2,2,768,128]{4,3,2,1,0:T(8,128)S(1)}, u32[]{:S(2)}) copy-start(f32[4,2,2,768,128]{4,3,2,1,0:T(8,128)S(1)} %halo.1.ext_ref) | copy-start | bytes 18874372
  46.9 2.8 %copy-start = (f32[4,2,2,768,128]{4,3,2,1,0:T(8,128)S(1)}, f32[4,2,2,768,128]{4,3,2,1,0:T(8,128)}, u32[]{:S(2)}) copy-start(f32[4,2,2,768,128]{4,3,2,1,0:T(8,128)} %get-tuple-element.7.gext_ref) | copy-start | bytes 18874372

commit v2 on v0

v2 whole, which is shorter than its diff:
```python
import functools
import math

import jax
import jax.numpy as jnp
import ml_dtypes
import numpy as np
from jax import lax
from jax.experimental import pallas as pl
from jax.experimental.pallas import tpu as pltpu
from jax.sharding import PartitionSpec as P

DEFOCUS = 0.3
FLOOR = 0.5


def real_form(m):
    return np.block([[m.real, -m.imag], [m.imag, m.real]])


def stage_matrices(window):
    half = window // 2
    index = np.arange(window)
    dft = np.exp(-2j * np.pi * (index[:, None] * index[None, :] % window) / window) / math.sqrt(window)
    freq = (index + half) % window - half
    phase = np.exp(-1j * np.pi * DEFOCUS * freq**2 / window)
    spread = dft.conj() @ (phase[:, None] * dft)
    near, far = spread[:half, :half], spread[:half, half:]
    stack = []
    for m in ((near + far) / 2, (near - far) / 2, dft[0::2, :half], dft[1::2, :half]):
        for form in (real_form(m), real_form(m).T):
            form = form.astype(np.float32)
            high = form.astype(ml_dtypes.bfloat16)
            low = (form - high.astype(np.float32)).astype(ml_dtypes.bfloat16)
            stack.append(np.concatenate([high, low], axis=1))
    return np.stack(stack)


PU, PU_T, PV, PV_T, FE, FE_T, FO, FO_T = range(8)


def split(x):
    high = x.astype(jnp.bfloat16)
    low = (x - high.astype(jnp.float32)).astype(jnp.bfloat16)
    return high, low


def dot(a, b):
    return jnp.dot(a, b, preferred_element_type=jnp.float32)


def from_left(w_ref, which, x):
    n = x.shape[0]
    high, low = split(x)
    wh, wl = w_ref[which, :, :n], w_ref[which, :, n:]
    return dot(wh, high) + dot(wh, low) + dot(wl, high)


def from_right(w_ref, which, x):
    n = x.shape[1]
    high, low = split(x)
    wh, wl = w_ref[which, :, :n], w_ref[which, :, n:]
    return dot(high, wh) + dot(low, wh) + dot(high, wl)


def rows(*parts):
    return jnp.concatenate(parts, axis=0)


def lanes(*parts):
    return jnp.concatenate(parts, axis=1)


def spread_field(w_ref, mats, xr, xi):
    u, v, ut, vt = mats
    h = xr.shape[0] // 2
    a = from_left(w_ref, u, rows(xr[:h] + xr[h:], xi[:h] + xi[h:]))
    b = from_left(w_ref, v, rows(xr[:h] - xr[h:], xi[:h] - xi[h:]))
    p, m = a + b, a - b
    yr, yi = rows(p[:h], m[:h]), rows(p[h:], m[h:])
    a = from_right(w_ref, ut, lanes(yr[:, :h] + yr[:, h:], yi[:, :h] + yi[:, h:]))
    b = from_right(w_ref, vt, lanes(yr[:, :h] - yr[:, h:], yi[:, :h] - yi[:, h:]))
    p, m = a + b, a - b
    return lanes(p[:, :h], m[:, :h]), lanes(p[:, h:], m[:, h:])


def to_far(w_ref, xr, xi):
    h = xr.shape[0] // 2
    e = from_left(w_ref, FE, rows(xr[:h] + xr[h:], xi[:h] + xi[h:]))
    o = from_left(w_ref, FO, rows(xr[:h] - xr[h:], xi[:h] - xi[h:]))
    yr, yi = rows(e[:h], o[:h]), rows(e[h:], o[h:])
    qe = from_right(w_ref, FE_T, lanes(yr[:, :h] + yr[:, h:], yi[:, :h] + yi[:, h:]))
    qo = from_right(w_ref, FO_T, lanes(yr[:, :h] - yr[:, h:], yi[:, :h] - yi[:, h:]))
    return qe, qo


def from_far(w_ref, ge, go):
    h = ge.shape[0] // 2
    a = from_right(w_ref, FE, ge)
    b = from_right(w_ref, FO, go)
    p, m = a + b, a - b
    yr, yi = lanes(p[:, :h], m[:, :h]), lanes(p[:, h:], m[:, h:])
    a = from_left(w_ref, FE_T, rows(yr[:h], yi[:h]))
    b = from_left(w_ref, FO_T, rows(yr[h:], yi[h:]))
    p, m = a + b, a - b
    return rows(p[:h], m[:h]), rows(p[h:], m[h:])


def one_hot(n, shift, across):
    a = lax.broadcasted_iota(jnp.int32, (n, n), 0)
    b = lax.broadcasted_iota(jnp.int32, (n, n), 1)
    gap = b - a - shift if across else a - b - shift
    return jnp.where((gap == 0) | (gap == -n), 1.0, 0.0).astype(jnp.bfloat16)


def take_left(m, x):
    high, low = split(x)
    return dot(m, high) + dot(m, low)


def take_right(x, m):
    high, low = split(x)
    return dot(high, m) + dot(low, m)


def move_probe(rs_ref, cs_ref, probe_ref, p_ref):
    n = probe_ref.shape[1]

    def one(s, carry):
        x = take_left(one_hot(n, lax.rem(rs_ref[s], n), False), lanes(probe_ref[0], probe_ref[1]))
        x = take_right(rows(x[:, :n], x[:, n:]), one_hot(n, lax.rem(cs_ref[s], n), True))
        p_ref[s, 0], p_ref[s, 1] = x[:n], x[n:]
        return carry

    lax.fori_loop(0, p_ref.shape[0], one, 0)


def far_order(meas_ref, m_ref):
    slots, n = meas_ref.shape[0], meas_ref.shape[1]
    h = n // 2
    lane = lax.broadcasted_iota(jnp.int32, (n, h), 1)
    pick = lax.rem(lane, h // 2) * 2

    def one(s, carry):
        for par in range(2):
            got = [jnp.take_along_axis(meas_ref[s, :, k * h : (k + 1) * h], pick + par, axis=1) for k in range(2)]
            m_ref[s, par] = jnp.where(lane < h // 2, got[0], got[1])
        return carry

    lax.fori_loop(0, slots, one, 0)


def cut_windows(layer, rs_ref, cs_ref, ext_ref, t_ref):
    slots, n = t_ref.shape[1], t_ref.shape[3]
    h = n // 2
    step = n // 4

    def one(i, carry):
        at = pl.multiple_of(i * step, step)
        row = lax.broadcasted_iota(jnp.int32, (step, h), 0) + at
        lane = lax.broadcasted_iota(jnp.int32, (step, h), 1)
        for part in range(2):
            for k in range(2):
                blocks = [[ext_ref[layer, 2 * w + k, part, pl.ds(m * n + at, step), :] for m in range(3)] for w in range(2)]
                for s in range(slots):
                    r, c = rs_ref[s], cs_ref[s]
                    halves = [jnp.where(row >= r, e[0], jnp.where(row >= r - n, e[1], e[2])) for e in blocks]
                    t_ref[layer, s, part, pl.ds(at, step), k * h : (k + 1) * h] = jnp.where(lane + k * h >= c, halves[0], halves[1])
        return carry

    lax.fori_loop(0, n // step, one, 0)


def forward(w_ref, p_ref, t_ref, psi_ref):
    def one(s, carry):
        pr, pi = p_ref[s, 0], p_ref[s, 1]
        tr, ti = t_ref[0, s, 0], t_ref[0, s, 1]
        psi_ref[s, 0], psi_ref[s, 1] = spread_field(w_ref, (PU, PV, PU_T, PV_T), tr * pr - ti * pi, tr * pi + ti * pr)
        return carry

    lax.fori_loop(0, t_ref.shape[1], one, 0, unroll=True)


def far_and_back(w_ref, count_ref, m_ref, t_ref, psi_ref, q_ref, patch_ref):
    h = t_ref.shape[3] // 2

    def one(s, carry):
        xr, xi = psi_ref[s, 0], psi_ref[s, 1]
        tr, ti = t_ref[1, s, 0], t_ref[1, s, 1]
        far = to_far(w_ref, tr * xr - ti * xi, tr * xi + ti * xr)
        live = jnp.where(s < count_ref[0], 1.0, 0.0).astype(jnp.float32)
        g = []
        for par, f in enumerate(far):
            fr, fi = f[:, :h], f[:, h:]
            inv = lax.rsqrt(jnp.maximum(fr * fr + fi * fi, FLOOR * FLOOR))
            amps = rows(*[m_ref[s, par, pl.ds(p, h, stride=2), :] for p in range(2)])
            weight = live * (1.0 - amps * inv)
            g.append(lanes(weight * fr, weight * fi))
        br, bi = from_far(w_ref, *g)
        xr, xi = psi_ref[s, 0], psi_ref[s, 1]
        patch_ref[s, 0] = xr * br + xi * bi
        patch_ref[s, 1] = xr * bi - xi * br
        tr, ti = t_ref[1, s, 0], t_ref[1, s, 1]
        q_ref[s, 0] = tr * br + ti * bi
        q_ref[s, 1] = tr * bi - ti * br
        return carry

    lax.fori_loop(0, t_ref.shape[1], one, 0, unroll=True)


def backward(w_ref, rs_ref, cs_ref, p_ref, t_ref, q_ref, patch_ref, pg_ref):
    n = t_ref.shape[3]
    h = n // 2
    pg_ref[...] = jnp.zeros_like(pg_ref)

    def one(s, carry):
        br, bi = spread_field(w_ref, (PU_T, PV_T, PU, PV), q_ref[s, 0], q_ref[s, 1])
        pr, pi = p_ref[s, 0], p_ref[s, 1]
        patch_ref[s, 0] = pr * br + pi * bi
        patch_ref[s, 1] = pr * bi - pi * br
        tr, ti = t_ref[0, s, 0], t_ref[0, s, 1]
        x = rows(tr * br + ti * bi, tr * bi - ti * br)
        x = take_right(x, one_hot(n, n - lax.rem(cs_ref[s], n), True))
        x = take_left(one_hot(n, n - lax.rem(rs_ref[s], n), False), lanes(x[:n], x[n:]))
        for part in range(2):
            for k in range(2):
                start = part * n + k * h
                spot = part, pl.ds(2 * k, 2)
                pg_ref[spot] += x[:, start : start + h].reshape((2,) + pg_ref.shape[2:])
        return carry

    lax.fori_loop(0, t_ref.shape[1], one, 0, unroll=True)


def add_patches(layer, rs_ref, cs_ref, patch_ref, gext_ref):
    slots, n = patch_ref.shape[0], patch_ref.shape[2]
    h = n // 2
    step = n // 8

    def one(i, carry):
        at = pl.multiple_of(i * step, step)
        row = lax.broadcasted_iota(jnp.int32, (step, h), 0) + at
        lane = lax.broadcasted_iota(jnp.int32, (step, h), 1)
        for part in range(2):
            for k in range(2):
                sums = [[None] * 3, [None] * 3]
                for s in range(slots):
                    r, c = rs_ref[s], cs_ref[s]
                    x = patch_ref[s, part, pl.ds(at, step), k * h : (k + 1) * h]
                    zero = jnp.zeros_like(x)
                    left = lane + k * h >= c
                    for w, y in enumerate((jnp.where(left, x, zero), jnp.where(left, zero, x))):
                        first, third = row >= r, row < r - n
                        parts = (jnp.where(first, y, zero), jnp.where(first | third, zero, y), jnp.where(third, y, zero))
                        for m in range(3):
                            sums[w][m] = parts[m] if sums[w][m] is None else sums[w][m] + parts[m]
                for w in range(2):
                    for m in range(3):
                        gext_ref[layer, 2 * w + k, part, pl.ds(m * n + at, step), :] = sums[w][m]
        return carry

    lax.fori_loop(0, n // step, one, 0)


MESH = pl.DeviceIdType.MESH
SIDES = ("up", "down", "left", "right")
OPPOSITE = {"up": "down", "down": "up", "left": "right", "right": "left"}


def step_kernel(rs_ref, cs_ref, count_ref, obj_hbm, probe_hbm, meas_hbm, w_hbm,
                grad_ref, total_ref,
                w_ref, probe_ref, meas_ref, ext_ref, gext_ref, t_ref, psi_ref, m_ref, q_ref, patch_ref, p_ref,
                corner_ref, side_ref, strip_ref, out_strip_ref,
                pg_ref, twin_ref, xs_ref, xr_ref, zs_ref, zr_ref, yr_ref, za_ref,
                local_sem, send_sem, recv_sem, sum_send, sum_recv):
    h = ext_ref.shape[4]
    tile = ext_ref.shape[3] - 2 * h
    row, col = lax.axis_index("row"), lax.axis_index("col")
    n_row, n_col = lax.axis_size("row"), lax.axis_size("col")
    near = {
        "up": (row > 0, {"row": row - 1, "col": col}),
        "down": (row < n_row - 1, {"row": row + 1, "col": col}),
        "left": (col > 0, {"row": row, "col": col - 1}),
        "right": (col < n_col - 1, {"row": row, "col": col + 1}),
    }
    y, x_hi = lax.rem(row, 4), lax.div(row, 4)
    core, z, x_lo = lax.rem(col, 2), lax.rem(lax.div(col, 2), 8), lax.div(col, 16)
    x = x_hi * 2 + x_lo
    twin = {"row": row, "col": col + 1 - 2 * core}

    def x_peer(k):
        other = lax.rem(x + k, 4)
        return {"row": lax.div(other, 2) * 4 + y, "col": lax.rem(other, 2) * 16 + z * 2 + core}

    def y_peer(k):
        return {"row": x_hi * 4 + lax.rem(y + k, 4), "col": col}

    def z_peer(k):
        return {"row": row, "col": x_lo * 16 + lax.rem(z + k, 8) * 2 + core}

    def send(number, src, dst, target, layer=None):
        sems = (sum_send.at[number], sum_recv.at[number]) if layer is None else (send_sem.at[layer, number], recv_sem.at[layer, number])
        return pltpu.make_async_remote_copy(src_ref=src, dst_ref=dst, send_sem=sems[0], recv_sem=sems[1], device_id=target, device_id_type=MESH)

    barrier = pltpu.get_barrier_semaphore()

    def greet(target):
        pl.semaphore_signal(barrier, inc=1, device_id=target, device_id_type=MESH)

    expected = 1 + 3 + 3 + 7
    for there, target in near.values():
        pl.when(there)(functools.partial(greet, target))
        expected = expected + jnp.where(there, 1, 0)
    for target in [twin] + [x_peer(k) for k in range(1, 4)] + [y_peer(k) for k in range(1, 4)] + [z_peer(k) for k in range(1, 8)]:
        greet(target)

    own = [pltpu.make_async_copy(meas_hbm, meas_ref, local_sem.at[0]),
           pltpu.make_async_copy(probe_hbm, probe_ref, local_sem.at[1]),
           pltpu.make_async_copy(w_hbm, w_ref, local_sem.at[2])]
    for layer in range(2):
        for b in range(2):
            own.append(pltpu.make_async_copy(obj_hbm.at[layer, :, :, pl.ds(b * h, h)], ext_ref.at[layer, 1 + b, :, pl.ds(h, tile), :], local_sem.at[3 + layer * 2 + b]))
    for c in own:
        c.start()
    own[0].wait()
    far_order(meas_ref, m_ref)
    own[1].wait()
    pl.semaphore_wait(barrier, expected)

    low = (0, tile + h)
    halo = [{}, {}]
    for layer in range(2):
        c = halo[layer]
        c[0] = "right", send(0, obj_hbm.at[layer, :, :, pl.ds(h, h)], ext_ref.at[layer, 0, :, pl.ds(h, tile), :], near["right"][1], layer)
        c[1] = "left", send(1, obj_hbm.at[layer, :, :, pl.ds(0, h)], ext_ref.at[layer, 3, :, pl.ds(h, tile), :], near["left"][1], layer)
        for b in range(2):
            c[2 + b] = "down", send(2 + b, obj_hbm.at[layer, :, pl.ds(tile - h, h), pl.ds(b * h, h)], ext_ref.at[layer, 1 + b, :, pl.ds(0, h), :], near["down"][1], layer)
            c[4 + b] = "up", send(4 + b, obj_hbm.at[layer, :, pl.ds(0, h), pl.ds(b * h, h)], ext_ref.at[layer, 1 + b, :, pl.ds(tile + h, h), :], near["up"][1], layer)
            for k in range(2):
                block = ext_ref.at[layer, 1 + b, :, pl.ds(low[k], h), :]
                side = ("left", "right")[b]
                c[6 + b * 2 + k] = side, send(6 + b * 2 + k, block, ext_ref.at[layer, (3, 0)[b], :, pl.ds(low[k], h), :], near[side][1], layer)

    def start(layer, numbers):
        for number in numbers:
            side, c = halo[layer][number]
            pl.when(near[side][0])(c.start)

    def forward_corners(layer):
        for b in range(2):
            for k in range(2):
                @pl.when(near[("up", "down")[k]][0])
                def _(b=b, k=k):
                    halo[layer][(2, 4)[k] + b][1].wait_recv()
                    start(layer, [6 + b * 2 + k])

    def halo_in(layer):
        own[3 + layer * 2].wait()
        own[4 + layer * 2].wait()
        for number in (0, 1, 6, 7, 8, 9):
            side, c = halo[layer][number]

            def arrive(side=side, c=c):
                pl.when(near[OPPOSITE[side]][0])(c.wait_recv)
            if number < 2:
                arrive()
            else:
                pl.when(near[("up", "down")[number % 2]][0])(arrive)

    start(0, (0, 1, 2, 3, 4, 5))
    start(1, (2, 3, 4, 5))
    forward_corners(0)
    start(1, (0, 1))
    move_probe(rs_ref, cs_ref, probe_ref, p_ref)
    own[2].wait()
    halo_in(0)
    cut_windows(0, rs_ref, cs_ref, ext_ref, t_ref)
    forward(w_ref, p_ref, t_ref, psi_ref)
    forward_corners(1)
    halo_in(1)
    cut_windows(1, rs_ref, cs_ref, ext_ref, t_ref)
    far_and_back(w_ref, count_ref, m_ref, t_ref, psi_ref, q_ref, patch_ref)
    add_patches(1, rs_ref, cs_ref, patch_ref, gext_ref)

    back = [{}, {}]
    for layer in range(2):
        for b, side in enumerate(("left", "right")):
            for k in range(2):
                number = 10 + b * 2 + k
                back[layer][number] = side, send(number, gext_ref.at[layer, b * 3, :, pl.ds(low[k], h), :], corner_ref.at[layer, b, k], near[side][1], layer)
            back[layer][14 + b] = side, send(14 + b, gext_ref.at[layer, b * 3, :, pl.ds(h, tile), :], side_ref.at[layer, b], near[side][1], layer)
        for k, side in enumerate(("up", "down")):
            for b in range(2):
                number = 16 + k * 2 + b
                back[layer][number] = side, send(number, out_strip_ref.at[layer, k, b], strip_ref.at[layer, k, b], near[side][1], layer)

    def start_back(layer, numbers):
        for number in numbers:
            side, c = back[layer][number]
            pl.when(near[side][0])(c.start)

    def strips_out(layer):
        for k in range(2):
            for b in range(2):
                out_strip_ref[layer, k, b] = gext_ref[layer, 1 + b, :, pl.ds(low[k], h), :]

                @pl.when(near[("left", "right")[b]][0])
                def _(k=k, b=b):
                    back[layer][10 + (1 - b) * 2 + k][1].wait_recv()
                    out_strip_ref[layer, k, b] += corner_ref[layer, 1 - b, k]
                start_back(layer, [16 + k * 2 + b])

    def join(layer):
        for b in range(2):
            where = pl.ds(b * h, h)
            grad_ref[layer, :, :, where] = gext_ref[layer, 1 + b, :, pl.ds(h, tile), :]

            @pl.when(near[("left", "right")[b]][0])
            def _(b=b, where=where):
                back[layer][14 + 1 - b][1].wait_recv()
                grad_ref[layer, :, :, where] += side_ref[layer, 1 - b]

            @pl.when(near["down"][0])
            def _(b=b, where=where):
                back[layer][16 + b][1].wait_recv()
                grad_ref[layer, :, pl.ds(tile - h, h), where] += strip_ref[layer, 0, b]

            @pl.when(near["up"][0])
            def _(b=b, where=where):
                back[layer][18 + b][1].wait_recv()
                grad_ref[layer, :, pl.ds(0, h), where] += strip_ref[layer, 1, b]

    start_back(1, range(10, 16))
    backward(w_ref, rs_ref, cs_ref, p_ref, t_ref, q_ref, patch_ref, pg_ref)

    sums = [send(0, pg_ref.at[1 - core], twin_ref, twin)]
    sums[0].start()
    add_patches(0, rs_ref, cs_ref, patch_ref, gext_ref)
    start_back(0, range(10, 14))
    sums[0].wait_recv()
    xs_ref[...] = pg_ref[core] + twin_ref[...]

    def exchange(copies):
        for c in copies:
            c.start()
        sums.extend(copies)
        return copies

    def arrive(copies):
        for c in copies:
            c.wait_recv()

    along_x = exchange([send(k, xs_ref.at[lax.rem(x + k, 4)], xr_ref.at[k - 1], x_peer(k)) for k in range(1, 4)])
    strips_out(1)
    arrive(along_x)
    zs_ref[...] = xs_ref[x] + xr_ref[0] + xr_ref[1] + xr_ref[2]
    along_z = exchange([send(3 + k, zs_ref.at[lax.rem(z + k, 8)], zr_ref.at[k - 1], z_peer(k)) for k in range(1, 8)])
    start_back(0, (14, 15))
    arrive(along_z)
    yr_ref[y] = zs_ref[z] + jnp.sum(zr_ref[...], axis=0)
    along_y = exchange([send(10 + k, yr_ref.at[y], yr_ref.at[y], y_peer(k)) for k in range(1, 4)])
    strips_out(0)
    arrive(along_y)
    za_ref[z] = yr_ref[0] + yr_ref[1] + yr_ref[2] + yr_ref[3]
    along_z = exchange([send(13 + k, za_ref.at[z], za_ref.at[z], z_peer(k)) for k in range(1, 8)])
    arrive(along_z)
    total_ref[core, x] = za_ref[...]
    along_x = exchange([send(20 + k, za_ref, total_ref.at[core, x], x_peer(k)) for k in range(1, 4)])
    join(1)
    arrive(along_x)
    last = exchange([send(24, total_ref.at[core], total_ref.at[core], twin)])
    join(0)
    arrive(last)

    for c in sums:
        c.wait_send()
    for layer in range(2):
        for number, (side, c) in list(halo[layer].items()) + list(back[layer].items()):
            def sent(side=side, c=c):
                pl.when(near[side][0])(c.wait_send)
            if 6 <= number < 10:
                pl.when(near[("up", "down")[number % 2]][0])(sent)
            else:
                sent()


def step(rs, cs, count, obj, probe, meas, w):
    layers, parts, tile, _ = obj.shape
    n = probe.shape[1]
    h = n // 2
    slots = meas.shape[0]
    smem, vmem, hbm = (pl.BlockSpec(memory_space=s) for s in (pltpu.SMEM, pltpu.VMEM, pltpu.HBM))
    f32 = jnp.float32
    shapes = [
        probe.shape, meas.shape,
        (layers, 4, parts, tile + n, h), (layers, 4, parts, tile + n, h),
        (layers, slots, parts, n, n), (slots, parts, n, n), (slots, 2, n, h), (slots, parts, n, n),
        (slots, parts, n, n), (slots, parts, n, n),
        (layers, 2, 2, parts, h, h), (layers, 2, parts, tile, h), (layers, 2, 2, parts, h, h), (layers, 2, 2, parts, h, h),
        (2, 4, 8, 16, 128), (4, 8, 16, 128), (4, 8, 16, 128), (3, 8, 16, 128), (8, 16, 128), (7, 16, 128), (4, 16, 128), (8, 16, 128),
    ]
    dma = pltpu.SemaphoreType.DMA
    return pl.pallas_call(
        step_kernel,
        out_shape=(jax.ShapeDtypeStruct(obj.shape, f32), jax.ShapeDtypeStruct((2, 4, 8, 16, 128), f32)),
        in_specs=[smem, smem, smem, hbm, hbm, hbm, hbm],
        out_specs=(vmem, vmem),
        scratch_shapes=[pltpu.VMEM(w.shape, w.dtype)] + [pltpu.VMEM(s, f32) for s in shapes]
        + [dma((7,)), dma((2, 20)), dma((2, 20)), dma((25,)), dma((25,))],
        compiler_params=pltpu.CompilerParams(collective_id=0, has_side_effects=True, vmem_limit_bytes=56 << 20),
        name="step",
    )(rs, cs, count, obj, probe, meas, w)


def local(w, object_slices, probe_field, scan_offsets, scan_count, measured):
    _, _, tile_rows, tile_cols = object_slices.shape
    n = probe_field.shape[1]
    rs = scan_offsets[0, 0, 0] - lax.axis_index("row") * tile_rows + n // 2
    cs = scan_offsets[0, 0, 1] - lax.axis_index("col") * tile_cols + n // 2
    object_grad, total = step(rs, cs, scan_count[0], object_slices, probe_field, measured[0, 0], w)
    positions = lax.axis_size("row") * lax.axis_size("col") * measured.shape[2]
    probe_grad = total.reshape(2, 2, n, n // 2).transpose(0, 2, 1, 3).reshape(2, n, n) / math.sqrt(positions)
    return object_grad, probe_grad


def solution(mesh):
    placed = (
        P(None, None, "row", "col"),
        P(),
        P("row", "col", None, None),
        P("row", "col"),
        P("row", "col", None, None, None),
    )
    w = stage_matrices(256)
    return jax.shard_map(
        lambda *args: local(jnp.asarray(w), *args),
        mesh=mesh,
        in_specs=placed,
        out_specs=(P(None, None, "row", "col"), P()),
        check_vma=False,
    )
```

time: 623 us -> 99.5 us (0.16)
  waiting for transfers between devices: 301 us -> 0 us
  matrix products: 139 us -> 0 us
  Pallas kernels: 0 us -> 93.4 us
  local copies, waits for them, and re-layouts: 91.2 us -> 2.16 us
  starting transfers between devices: 30.9 us -> 0 us
  other arithmetic: 24.2 us -> 2.5 us
  loops' own time: 15.8 us -> 0 us
  between operations: 15.6 us -> 1.3 us
    psum x1 -> x0, waiting for transfers between devices: 262 us -> none  [local(): probe_total = lax.psum(probe_term, ('row', 'col'))]
    dot_general x48 -> x0, matrix products: 139 us -> none  [the longest x6 18.2 us: transform(): jnp.einsum('jk,skl->sjl', c_re, x_re, precision=highest)]
    pallas_call x0 -> x1, Pallas kernels: none -> 93.4 us  [step(): pl.pallas_call(step_kernel, out_shape=(jax.ShapeDtypeStruct(obj.shape, f3...]
    dynamic_update_slice x4 -> x0, local copies, waits for them, and re-layouts: 47.8 us -> none  [place_slot(): lax.dynamic_update_slice(accumulated, current + patch_grads[slot_index],...]
    ppermute x8 -> x0, waiting for transfers between devices: 38.7 us -> none  [the longest x2 20.3 us: with_halo(): before = lax.ppermute(last, axis, up)]
    ppermute x8 -> x0, starting transfers between devices: 30.8 us -> none  [the longest x4 18.3 us: passed_along(): return lax.ppermute(block, axis, route)]
    gather x12 -> x0, local copies, waits for them, and re-layouts: 18.6 us -> none
    another operation x2 -> x0, loops' own time: 15.8 us -> none  [the longest x1 15.6 us: local(): extended_grad = lax.fori_loop(0, slot_count, place_slot, start_grad)]
  transfers between devices with their start and end apart: 9 -> 0, of which waited for: 7 -> 0; matrix products, arithmetic and copies ran while one was open for 2% -> 0% of each run, Pallas kernels for 0% -> 0%
where the time goes in v2:
time: 99.5 us; the launch traced here: 99.3 us
  Pallas kernels  93.4 us (94%)
  other arithmetic  2.5 us (3%)
  local copies, waits for them, and re-layouts  2.16 us (2%)
  between operations  1.3 us (1%)
    pallas_call x1, Pallas kernels, step(): pl.pallas_call(step_kernel, out_shape=(jax.ShapeDtypeStruct(obj.shape, f3...  93.4 us

profile of v2, /device:TPU:1, one launch (start us, length us, event | category | flops | bytes accessed | tf_op | source)
XLA Modules:
  0.0 99.3 jit_solution(12592315459553083662)
XLA Ops:
  1.3 1.3 %add_bitcast_fusion = (s32[4]{0:T(128)}, s32[4]{0:T(128)}) fusion(s32[1,1,2,4]{3,2,1,0:T(2,128)} %param.8, s32[]{:T(128)S(6)} %mul.7, s32[]{:T(128)S(6)} %mul.6), kind=kLoop, calls=%fused_computation.2 | loop fusion | flops 16 | bytes 72 | tf_op jit(solution)/shard_map/add | solution.py:519
  2.6 93.4 %step.1 = (f32[2,2,512,256]{3,2,1,0:T(8,128)}, f32[2,4,8,16,128]{4,3,2,1,0:T(8,128)}) custom-call(s32[4]{0:T(128)} %get-tuple-element.7.rs_ref, s32[4]{0:T(128)} %get-tuple-element.6.cs_ref, s32[1]{0:T(128)} %bitcast.13.count_ref, f32[2,2,512,256]{3,2,1,0:T(8,128)} %obj_hbm.1, f32[2,256,256]{2,1,0:T(8,128)} %probe_hbm.1, f32[4,256,256]{2,1,0:T(8,128)} %bitcast.15, ...), custom_call_target="tpu_custom_call" | custom-call | tf_op jit(solution)/shard_map/step/pallas_call | solution.py:503
  95.9 0.0 copy-start
  95.9 1.2 %broadcast_multiply_fusion = f32[2,4,8,16,128]{4,3,2,1,0:T(8,128)S(1)} fusion(f32[2,4,8,16,128]{4,3,2,1,0:T(8,128)} %get-tuple-element.5), kind=kLoop, calls=%fused_computation.1 | loop fusion | flops 131072 | bytes 1048576 | tf_op jit(solution)/shard_map/div | solution.py:522
  97.2 0.8 copy.11
  98.0 0.0 copy-done
  98.0 1.3 %copy.14 = f32[2,2,512,256]{3,2,1,0:T(8,128)} copy(f32[2,2,512,256]{3,2,1,0:T(8,128)S(1)} %copy-done) | data formatting | bytes 4194304
Async XLA Ops:
  95.9 2.1 %copy-start = (f32[2,2,512,256]{3,2,1,0:T(8,128)S(1)}, f32[2,2,512,256]{3,2,1,0:T(8,128)}, u32[]{:S(2)}) copy-start(f32[2,2,512,256]{3,2,1,0:T(8,128)} %get-tuple-element.10) | copy-start | bytes 6291460

commit v3 on v2

--- a/solution.py
+++ b/solution.py
@@ -132,7 +132,8 @@
         p_ref[s, 0], p_ref[s, 1] = x[:n], x[n:]
         return carry
 
-    lax.fori_loop(0, p_ref.shape[0], one, 0)
+    for s in range(p_ref.shape[0]):
+        one(s, 0)
 
 
 def far_order(meas_ref, m_ref):
@@ -178,23 +179,23 @@
         psi_ref[s, 0], psi_ref[s, 1] = spread_field(w_ref, (PU, PV, PU_T, PV_T), tr * pr - ti * pi, tr * pi + ti * pr)
         return carry
 
-    lax.fori_loop(0, t_ref.shape[1], one, 0, unroll=True)
-
-
-def far_and_back(w_ref, count_ref, m_ref, t_ref, psi_ref, q_ref, patch_ref):
+    for s in range(t_ref.shape[1]):
+        one(s, 0)
+
+
+def far_and_back(w_ref, live, m_ref, t_ref, psi_ref, q_ref, patch_ref):
     h = t_ref.shape[3] // 2
 
     def one(s, carry):
         xr, xi = psi_ref[s, 0], psi_ref[s, 1]
         tr, ti = t_ref[1, s, 0], t_ref[1, s, 1]
         far = to_far(w_ref, tr * xr - ti * xi, tr * xi + ti * xr)
-        live = jnp.where(s < count_ref[0], 1.0, 0.0).astype(jnp.float32)
         g = []
         for par, f in enumerate(far):
             fr, fi = f[:, :h], f[:, h:]
             inv = lax.rsqrt(jnp.maximum(fr * fr + fi * fi, FLOOR * FLOOR))
             amps = rows(*[m_ref[s, par, pl.ds(p, h, stride=2), :] for p in range(2)])
-            weight = live * (1.0 - amps * inv)
+            weight = live[s] * (1.0 - amps * inv)
             g.append(lanes(weight * fr, weight * fi))
         br, bi = from_far(w_ref, *g)
         xr, xi = psi_ref[s, 0], psi_ref[s, 1]
@@ -205,12 +206,12 @@
         q_ref[s, 1] = tr * bi - ti * br
         return carry
 
-    lax.fori_loop(0, t_ref.shape[1], one, 0, unroll=True)
+    for s in range(t_ref.shape[1]):
+        one(s, 0)
 
 
 def backward(w_ref, rs_ref, cs_ref, p_ref, t_ref, q_ref, patch_ref, pg_ref):
     n = t_ref.shape[3]
-    h = n // 2
     pg_ref[...] = jnp.zeros_like(pg_ref)
 
     def one(s, carry):
@@ -223,13 +224,11 @@
         x = take_right(x, one_hot(n, n - lax.rem(cs_ref[s], n), True))
         x = take_left(one_hot(n, n - lax.rem(rs_ref[s], n), False), lanes(x[:n], x[n:]))
         for part in range(2):
-            for k in range(2):
-                start = part * n + k * h
-                spot = part, pl.ds(2 * k, 2)
-                pg_ref[spot] += x[:, start : start + h].reshape((2,) + pg_ref.shape[2:])
-        return carry
-
-    lax.fori_loop(0, t_ref.shape[1], one, 0, unroll=True)
+            pg_ref[part] += x[:, part * n : (part + 1) * n].reshape(pg_ref.shape[1:])
+        return carry
+
+    for s in range(t_ref.shape[1]):
+        one(s, 0)
 
 
 def add_patches(layer, rs_ref, cs_ref, patch_ref, gext_ref):
@@ -267,9 +266,9 @@
 OPPOSITE = {"up": "down", "down": "up", "left": "right", "right": "left"}
 
 
-def step_kernel(rs_ref, cs_ref, count_ref, obj_hbm, probe_hbm, meas_hbm, w_hbm,
+def step_kernel(scale, offsets_hbm, count_hbm, obj_hbm, probe_hbm, meas_hbm, w_hbm,
                 grad_ref, total_ref,
-                w_ref, probe_ref, meas_ref, ext_ref, gext_ref, t_ref, psi_ref, m_ref, q_ref, patch_ref, p_ref,
+                offsets_ref, count_ref, w_ref, probe_ref, meas_ref, ext_ref, gext_ref, t_ref, psi_ref, m_ref, q_ref, patch_ref, p_ref,
                 corner_ref, side_ref, strip_ref, out_strip_ref,
                 pg_ref, twin_ref, xs_ref, xr_ref, zs_ref, zr_ref, yr_ref, za_ref,
                 local_sem, send_sem, recv_sem, sum_send, sum_recv):
@@ -317,18 +316,38 @@
     own = [pltpu.make_async_copy(meas_hbm, meas_ref, local_sem.at[0]),
            pltpu.make_async_copy(probe_hbm, probe_ref, local_sem.at[1]),
            pltpu.make_async_copy(w_hbm, w_ref, local_sem.at[2])]
+    small = [pltpu.make_async_copy(offsets_hbm, offsets_ref, local_sem.at[7]), pltpu.make_async_copy(count_hbm, count_ref, local_sem.at[8])]
+    for c in small:
+        c.start()
     for layer in range(2):
         for b in range(2):
             own.append(pltpu.make_async_copy(obj_hbm.at[layer, :, :, pl.ds(b * h, h)], ext_ref.at[layer, 1 + b, :, pl.ds(h, tile), :], local_sem.at[3 + layer * 2 + b]))
     for c in own:
         c.start()
-    own[0].wait()
+    got_own = set()
+
+    def wait_own(i):
+        if i not in got_own:
+            got_own.add(i)
+            own[i].wait()
+
+    got = set()
+    wait_own(0)
     far_order(meas_ref, m_ref)
-    own[1].wait()
+    for c in small:
+        c.wait()
+    rs = [offsets_ref[0, 0, 0, i] - row * tile + h for i in range(4)]
+    cs = [offsets_ref[0, 0, 1, i] - col * (2 * h) + h for i in range(4)]
+    live = [jnp.where(i < count_ref[0, 0], 1.0, 0.0).astype(jnp.float32) for i in range(4)]
+    wait_own(1)
+    move_probe(rs, cs, probe_ref, p_ref)
     pl.semaphore_wait(barrier, expected)
 
+    sums = []
+    back = [{}, {}]
     low = (0, tile + h)
     halo = [{}, {}]
+    begun = set()
     for layer in range(2):
         c = halo[layer]
         c[0] = "right", send(0, obj_hbm.at[layer, :, :, pl.ds(h, h)], ext_ref.at[layer, 0, :, pl.ds(h, tile), :], near["right"][1], layer)
@@ -341,12 +360,16 @@
                 side = ("left", "right")[b]
                 c[6 + b * 2 + k] = side, send(6 + b * 2 + k, block, ext_ref.at[layer, (3, 0)[b], :, pl.ds(low[k], h), :], near[side][1], layer)
 
+    def begin(layer, number, side, c):
+        begun.add((layer, number))
+        pl.when(near[side][0])(c.start)
+
     def start(layer, numbers):
         for number in numbers:
-            side, c = halo[layer][number]
-            pl.when(near[side][0])(c.start)
+            begin(layer, number, *halo[layer][number])
 
     def forward_corners(layer):
+        got.update((layer, i) for i in (2, 3, 4, 5))
         for b in range(2):
             for k in range(2):
                 @pl.when(near[("up", "down")[k]][0])
@@ -355,8 +378,9 @@
                     start(layer, [6 + b * 2 + k])
 
     def halo_in(layer):
-        own[3 + layer * 2].wait()
-        own[4 + layer * 2].wait()
+        got.update((layer, i) for i in (0, 1, 6, 7, 8, 9))
+        wait_own(3 + layer * 2)
+        wait_own(4 + layer * 2)
         for number in (0, 1, 6, 7, 8, 9):
             side, c = halo[layer][number]
 
@@ -367,20 +391,18 @@
             else:
                 pl.when(near[("up", "down")[number % 2]][0])(arrive)
 
-    start(0, (0, 1, 2, 3, 4, 5))
-    start(1, (2, 3, 4, 5))
+    start(0, (2, 3, 4, 5, 0, 1))
     forward_corners(0)
-    start(1, (0, 1))
-    move_probe(rs_ref, cs_ref, probe_ref, p_ref)
-    own[2].wait()
+    wait_own(2)
     halo_in(0)
-    cut_windows(0, rs_ref, cs_ref, ext_ref, t_ref)
+    start(1, (2, 3, 4, 5, 0, 1))
+    cut_windows(0, rs, cs, ext_ref, t_ref)
     forward(w_ref, p_ref, t_ref, psi_ref)
     forward_corners(1)
     halo_in(1)
-    cut_windows(1, rs_ref, cs_ref, ext_ref, t_ref)
-    far_and_back(w_ref, count_ref, m_ref, t_ref, psi_ref, q_ref, patch_ref)
-    add_patches(1, rs_ref, cs_ref, patch_ref, gext_ref)
+    cut_windows(1, rs, cs, ext_ref, t_ref)
+    far_and_back(w_ref, live, m_ref, t_ref, psi_ref, q_ref, patch_ref)
+    add_patches(1, rs, cs, patch_ref, gext_ref)
 
     back = [{}, {}]
     for layer in range(2):
@@ -396,10 +418,10 @@
 
     def start_back(layer, numbers):
         for number in numbers:
-            side, c = back[layer][number]
-            pl.when(near[side][0])(c.start)
+            begin(layer, number, *back[layer][number])
 
     def strips_out(layer):
+        got.update((layer, i) for i in (10, 11, 12, 13))
         for k in range(2):
             for b in range(2):
                 out_strip_ref[layer, k, b] = gext_ref[layer, 1 + b, :, pl.ds(low[k], h), :]
@@ -411,6 +433,7 @@
                 start_back(layer, [16 + k * 2 + b])
 
     def join(layer):
+        got.update((layer, i) for i in range(14, 20))
         for b in range(2):
             where = pl.ds(b * h, h)
             grad_ref[layer, :, :, where] = gext_ref[layer, 1 + b, :, pl.ds(h, tile), :]
@@ -431,12 +454,12 @@
                 grad_ref[layer, :, pl.ds(0, h), where] += strip_ref[layer, 1, b]
 
     start_back(1, range(10, 16))
-    backward(w_ref, rs_ref, cs_ref, p_ref, t_ref, q_ref, patch_ref, pg_ref)
-
-    sums = [send(0, pg_ref.at[1 - core], twin_ref, twin)]
+    backward(w_ref, rs, cs, p_ref, t_ref, q_ref, patch_ref, pg_ref)
+
+    sums[:] = [send(0, pg_ref.at[1 - core], twin_ref, twin)]
     sums[0].start()
-    add_patches(0, rs_ref, cs_ref, patch_ref, gext_ref)
-    start_back(0, range(10, 14))
+    strips_out(1)
+    got.add(id(sums[0]))
     sums[0].wait_recv()
     xs_ref[...] = pg_ref[core] + twin_ref[...]
 
@@ -448,10 +471,12 @@
 
     def arrive(copies):
         for c in copies:
+            got.add(id(c))
             c.wait_recv()
 
     along_x = exchange([send(k, xs_ref.at[lax.rem(x + k, 4)], xr_ref.at[k - 1], x_peer(k)) for k in range(1, 4)])
-    strips_out(1)
+    add_patches(0, rs, cs, patch_ref, gext_ref)
+    start_back(0, range(10, 14))
     arrive(along_x)
     zs_ref[...] = xs_ref[x] + xr_ref[0] + xr_ref[1] + xr_ref[2]
     along_z = exchange([send(3 + k, zs_ref.at[lax.rem(z + k, 8)], zr_ref.at[k - 1], z_peer(k)) for k in range(1, 8)])
@@ -461,7 +486,7 @@
     along_y = exchange([send(10 + k, yr_ref.at[y], yr_ref.at[y], y_peer(k)) for k in range(1, 4)])
     strips_out(0)
     arrive(along_y)
-    za_ref[z] = yr_ref[0] + yr_ref[1] + yr_ref[2] + yr_ref[3]
+    za_ref[z] = (yr_ref[0] + yr_ref[1] + yr_ref[2] + yr_ref[3]) * scale
     along_z = exchange([send(13 + k, za_ref.at[z], za_ref.at[z], z_peer(k)) for k in range(1, 8)])
     arrive(along_z)
     total_ref[core, x] = za_ref[...]
@@ -472,10 +497,29 @@
     join(0)
     arrive(last)
 
+    for i in range(7):
+        wait_own(i)
+    for c in sums:
+        if id(c) not in got:
+            c.wait_recv()
+    for layer in range(2):
+        for number, (side, c) in list(halo[layer].items()) + list(back[layer].items()):
+            if (layer, number) in begun and (layer, number) not in got:
+                def came(side=side, c=c):
+                    pl.when(near[OPPOSITE[side]][0])(c.wait_recv)
+                if 6 <= number < 10:
+                    pl.when(near[("up", "down")[number % 2]][0])(came)
+                else:
+                    came()
     for c in sums:
         c.wait_send()
     for layer in range(2):
+        pass
+    for layer in range(2):
         for number, (side, c) in list(halo[layer].items()) + list(back[layer].items()):
+            if (layer, number) not in begun:
+                continue
+
             def sent(side=side, c=c):
                 pl.when(near[side][0])(c.wait_send)
             if 6 <= number < 10:
@@ -484,12 +528,12 @@
                 sent()
 
 
-def step(rs, cs, count, obj, probe, meas, w):
+def step(scale, offsets, count, obj, probe, meas, w):
     layers, parts, tile, _ = obj.shape
     n = probe.shape[1]
     h = n // 2
     slots = meas.shape[0]
-    smem, vmem, hbm = (pl.BlockSpec(memory_space=s) for s in (pltpu.SMEM, pltpu.VMEM, pltpu.HBM))
+    vmem, hbm = (pl.BlockSpec(memory_space=s) for s in (pltpu.VMEM, pltpu.HBM))
     f32 = jnp.float32
     shapes = [
         probe.shape, meas.shape,
@@ -497,30 +541,26 @@
         (layers, slots, parts, n, n), (slots, parts, n, n), (slots, 2, n, h), (slots, parts, n, n),
         (slots, parts, n, n), (slots, parts, n, n),
         (layers, 2, 2, parts, h, h), (layers, 2, parts, tile, h), (layers, 2, 2, parts, h, h), (layers, 2, 2, parts, h, h),
-        (2, 4, 8, 16, 128), (4, 8, 16, 128), (4, 8, 16, 128), (3, 8, 16, 128), (8, 16, 128), (7, 16, 128), (4, 16, 128), (8, 16, 128),
+        (2, 4, 8, 8, n), (4, 8, 8, n), (4, 8, 8, n), (3, 8, 8, n), (8, 8, n), (7, 8, n), (4, 8, n), (8, 8, n),
     ]
     dma = pltpu.SemaphoreType.DMA
     return pl.pallas_call(
-        step_kernel,
-        out_shape=(jax.ShapeDtypeStruct(obj.shape, f32), jax.ShapeDtypeStruct((2, 4, 8, 16, 128), f32)),
-        in_specs=[smem, smem, smem, hbm, hbm, hbm, hbm],
+        functools.partial(step_kernel, scale),
+        out_shape=(jax.ShapeDtypeStruct(obj.shape, f32), jax.ShapeDtypeStruct((2, 4, 8, 8, n), f32)),
+        in_specs=[hbm] * 6,
         out_specs=(vmem, vmem),
-        scratch_shapes=[pltpu.VMEM(w.shape, w.dtype)] + [pltpu.VMEM(s, f32) for s in shapes]
-        + [dma((7,)), dma((2, 20)), dma((2, 20)), dma((25,)), dma((25,))],
-        compiler_params=pltpu.CompilerParams(collective_id=0, has_side_effects=True, vmem_limit_bytes=56 << 20),
+        scratch_shapes=[pltpu.SMEM(offsets.shape, jnp.int32), pltpu.SMEM(count.shape, jnp.int32), pltpu.VMEM(w.shape, w.dtype)] + [pltpu.VMEM(s, f32) for s in shapes]
+        + [dma((9,)), dma((2, 20)), dma((2, 20)), dma((25,)), dma((25,))],
+        compiler_params=pltpu.CompilerParams(collective_id=0, has_side_effects=True, vmem_limit_bytes=46 << 20),
         name="step",
-    )(rs, cs, count, obj, probe, meas, w)
+    )(offsets, count, *(pltpu.with_memory_space_constraint(a, pltpu.HBM) for a in (obj, probe, meas, w)))
 
 
 def local(w, object_slices, probe_field, scan_offsets, scan_count, measured):
-    _, _, tile_rows, tile_cols = object_slices.shape
-    n = probe_field.shape[1]
-    rs = scan_offsets[0, 0, 0] - lax.axis_index("row") * tile_rows + n // 2
-    cs = scan_offsets[0, 0, 1] - lax.axis_index("col") * tile_cols + n // 2
-    object_grad, total = step(rs, cs, scan_count[0], object_slices, probe_field, measured[0, 0], w)
     positions = lax.axis_size("row") * lax.axis_size("col") * measured.shape[2]
-    probe_grad = total.reshape(2, 2, n, n // 2).transpose(0, 2, 1, 3).reshape(2, n, n) / math.sqrt(positions)
-    return object_grad, probe_grad
+    scale = 1.0 / math.sqrt(positions)
+    object_grad, total = step(scale, scan_offsets, scan_count, object_slices, probe_field, measured[0, 0], w)
+    return object_grad, total.reshape(probe_field.shape)
 
 
 def solution(mesh):

time: 99.5 us -> 95 us (0.955)
  Pallas kernels: 93.4 us -> 90.8 us
  other arithmetic: 2.5 us -> 0 us
    pallas_call x1, Pallas kernels: 93.4 us -> 90.8 us  [step(): pl.pallas_call(functools.partial(step_kernel, scale), out_shape=(jax.Shap...]
    unnamed x3 -> x4, local copies, waits for them, and re-layouts: 1.32 us -> 2.79 us
    add x1 -> x0, other arithmetic: 1.28 us -> none  [local(): cs = scan_offsets[0, 0, 1] - lax.axis_index('col') * tile_cols + n // 2]
    div x1 -> x0, other arithmetic: 1.23 us -> none  [local(): total.reshape(2, 2, n, n // 2).transpose(0, 2, 1, 3).reshape(2, n, n)]
where the time goes in v3:
time: 95 us; the launch traced here: 94.9 us
  Pallas kernels  90.8 us (96%)
  local copies, waits for them, and re-layouts  2.79 us (3%)
  between operations  1.29 us (1%)
    pallas_call x1, Pallas kernels, step(): pl.pallas_call(functools.partial(step_kernel, scale), out_shape=(jax.Shap...  90.8 us
    unnamed x4, local copies, waits for them, and re-layouts  2.79 us

profile of v3, /device:TPU:1, one launch (start us, length us, event | category | flops | bytes accessed | tf_op | source)
XLA Modules:
  0.0 94.9 jit_solution(7751569452590930801)
XLA Ops:
  1.3 0.0 copy-start
  1.3 0.7 copy-done
  2.0 90.8 %step.1 = (f32[2,2,512,256]{3,2,1,0:T(8,128)S(1)}, f32[2,4,8,8,256]{4,3,2,1,0:T(8,128)S(1)}) custom-call(s32[1,1,2,4]{3,2,1,0:T(2,128)S(1)} %copy-done, s32[1,1]{1,0:T(1,128)S(6)} %copy.10.count_hbm, f32[2,2,512,256]{3,2,1,0:T(8,128)} %obj_hbm.1, f32[2,256,256]{2,1,0:T(8,128)} %probe_hbm.1, f32[4,256,256]{2,1,0:T(8,128)} %bitcast.3, ...), custom_call_target="tpu_custom_call" | custom-call | tf_op jit(solution)/shard_map/step/pallas_call | solution.py:547
  92.8 1.3 %copy.11 = f32[2,2,512,256]{3,2,1,0:T(8,128)} copy(f32[2,2,512,256]{3,2,1,0:T(8,128)S(1)} %get-tuple-element.8) | data formatting | bytes 4194304
  94.1 0.8 copy.12
Async XLA Ops:
  1.3 0.7 copy-start

commit v4 on v3

--- a/solution.py
+++ b/solution.py
@@ -480,10 +480,10 @@
     arrive(along_x)
     zs_ref[...] = xs_ref[x] + xr_ref[0] + xr_ref[1] + xr_ref[2]
     along_z = exchange([send(3 + k, zs_ref.at[lax.rem(z + k, 8)], zr_ref.at[k - 1], z_peer(k)) for k in range(1, 8)])
-    start_back(0, (14, 15))
     arrive(along_z)
     yr_ref[y] = zs_ref[z] + jnp.sum(zr_ref[...], axis=0)
     along_y = exchange([send(10 + k, yr_ref.at[y], yr_ref.at[y], y_peer(k)) for k in range(1, 4)])
+    start_back(0, (14, 15))
     strips_out(0)
     arrive(along_y)
     za_ref[z] = (yr_ref[0] + yr_ref[1] + yr_ref[2] + yr_ref[3]) * scale

time: 95 us -> 94.9 us (level)
  no operation moved by 1% of the time
where the time goes in v4:
time: 94.9 us; the launch traced here: 94.7 us
  Pallas kernels  90.7 us (96%)
  local copies, waits for them, and re-layouts  2.79 us (3%)
  between operations  1.29 us (1%)
    pallas_call x1, Pallas kernels, step(): pl.pallas_call(functools.partial(step_kernel, scale), out_shape=(jax.Shap...  90.7 us
    unnamed x4, local copies, waits for them, and re-layouts  2.79 us

profile of v4, /device:TPU:1, one launch (start us, length us, event | category | flops | bytes accessed | tf_op | source)
XLA Modules:
  0.0 94.7 jit_solution(17783447255334339267)
XLA Ops:
  1.3 0.0 copy-start
  1.3 0.7 copy-done
  2.0 90.7 %step.1 = (f32[2,2,512,256]{3,2,1,0:T(8,128)S(1)}, f32[2,4,8,8,256]{4,3,2,1,0:T(8,128)S(1)}) custom-call(s32[1,1,2,4]{3,2,1,0:T(2,128)S(1)} %copy-done, s32[1,1]{1,0:T(1,128)S(6)} %copy.10.count_hbm, f32[2,2,512,256]{3,2,1,0:T(8,128)} %obj_hbm.1, f32[2,256,256]{2,1,0:T(8,128)} %probe_hbm.1, f32[4,256,256]{2,1,0:T(8,128)} %bitcast.3, ...), custom_call_target="tpu_custom_call" | custom-call | tf_op jit(solution)/shard_map/step/pallas_call | solution.py:547
  92.6 1.3 %copy.11 = f32[2,2,512,256]{3,2,1,0:T(8,128)} copy(f32[2,2,512,256]{3,2,1,0:T(8,128)S(1)} %get-tuple-element.8) | data formatting | bytes 4194304
  94.0 0.8 copy.12
Async XLA Ops:
  1.3 0.7 copy-start
